TPU v7x, 256 devices: a whole 4x4x8 slice. The times are simulated.
256 devices in a mesh: inline: 16 (over y, z_hi, core), crosslin: 16 (over x, z_lo).
Axes of the slice: x: 4, y: 4, z: 8 (z_hi: 2, z_lo: 4; z = z_hi * 4 + z_lo), core: 2. Of those that a mesh axis runs over, the one named last changes fastest.
Arguments:
- features: bfloat16 [32, 128, 256, 128], P(None, 'inline', 'crosslin'), may hold values from -6 to 6
- first_dilated_weight: bfloat16 [3, 3, 3, 32, 32], replicated, may hold values from -0.3125 to 0.3125
- first_dilated_bias: float32 [32], replicated, may hold values from -3 to 3
- second_dilated_weight: bfloat16 [3, 3, 3, 32, 32], replicated, may hold values from -0.3125 to 0.3125
- second_dilated_bias: float32 [32], replicated, may hold values from -3 to 3
- w_last: bfloat16 [3, 3, 3, 32], replicated, may hold values from -0.4375 to 0.4375
- b_last: float32 [1], replicated, may hold values from -3 to 3
Outputs:
- fault: float32 [128, 256, 128], P('inline', 'crosslin')
All inputs are finite; a program needn't handle non-finite values.
Results may differ from a plain program's by a relative error of at most 0.0026.
Values may be sent and summed in bfloat16 or wider, within the bound.
No kernel may reach another device: no remote copies, remote signals or barrier semaphores. Data moves between devices by JAX's collectives and lax.ppermute only.
A program may use at most 64 MiB of HBM per device.

v0:
```python
import jax
import jax.numpy as jnp
from jax import lax
from jax.sharding import PartitionSpec as P

DILATION_RATE = 8


def with_halo(cells, sides, width):
    for axis, dim in sides:
        count = lax.axis_size(axis)
        ends = count - 1
        head = lax.slice_in_dim(cells, 0, width, axis=dim)
        tail = lax.slice_in_dim(cells, cells.shape[dim] - width, cells.shape[dim], axis=dim)
        cells = jnp.concatenate(
            [
                lax.ppermute(tail, axis, [(i, (i + 1) % count) for i in range(ends)]),
                cells,
                lax.ppermute(head, axis, [((i + 1) % count, i) for i in range(ends)]),
            ],
            axis=dim,
        )
    return cells


def depth_stack(window, tap_spacing, depth):
    padded = jnp.pad(window, ((0, 0), (0, 0), (0, 0), (tap_spacing, tap_spacing)))
    return jnp.concatenate(
        [padded[..., step * tap_spacing : step * tap_spacing + depth] for step in range(3)], axis=0
    )


def conv_layer(pick, weight, bias, tap_spacing, depth):
    outputs = weight.shape[3]
    summed = None
    for offset_x in range(3):
        for offset_y in range(3):
            stacked = depth_stack(pick(offset_x, offset_y), tap_spacing, depth)
            matrix = jnp.transpose(weight[offset_x, offset_y], (1, 0, 2)).reshape(outputs, -1)
            product = jnp.einsum(
                "ok,kxyz->oxyz", matrix, stacked, preferred_element_type=jnp.float32
            )
            summed = product if summed is None else summed + product
    return jax.nn.relu(summed + bias[:, None, None, None]).astype(jnp.bfloat16)


def on_device(
    features,
    first_dilated_weight,
    first_dilated_bias,
    second_dilated_weight,
    second_dilated_bias,
    w_last,
    b_last,
):
    tap_spacing = DILATION_RATE
    rows = features.shape[1]
    columns_count = features.shape[2]
    depth = features.shape[3]
    layers = (
        (first_dilated_weight, first_dilated_bias),
        (second_dilated_weight, second_dilated_bias),
    )
    current = features
    for weight, bias in layers:
        wide = with_halo(current, (("inline", 1), ("crosslin", 2)), tap_spacing)

        def pick(offset_x, offset_y, wide=wide):
            return wide[
                :,
                offset_x * tap_spacing : offset_x * tap_spacing + rows,
                offset_y * tap_spacing : offset_y * tap_spacing + columns_count,
            ]

        current = conv_layer(pick, weight, bias, tap_spacing, depth)
    border = with_halo(current, (("inline", 1), ("crosslin", 2)), 1)
    logit = None
    for offset_x in range(3):
        for offset_y in range(3):
            window = border[:, offset_x : offset_x + rows, offset_y : offset_y + columns_count]
            stacked = depth_stack(window, 1, depth)
            vector = w_last[offset_x, offset_y].reshape(-1)
            product = jnp.einsum("k,kxyz->xyz", vector, stacked, preferred_element_type=jnp.float32)
            logit = product if logit is None else logit + product
    return jax.nn.sigmoid(logit + b_last[0])


def solution(mesh):
    return jax.shard_map(
        on_device,
        mesh=mesh,
        in_specs=(P(None, "inline", "crosslin", None), P(), P(), P(), P(), P(), P()),
        out_specs=P("inline", "crosslin", None),
        check_vma=False,
    )
```

profile of v0, /device:TPU:11, one launch (start us, length us, event | category | flops | bytes accessed | tf_op | source)
XLA Modules:
  0.0 332.0 jit_solution(725366616331084207)
XLA Ops:
  0.0 2.0 copy.31
  2.0 9.4 %collective-permute-start = (bf16[32,8,16,128]{3,0,2,1:T(8,128)(2,1)S(1)}, bf16[32,8,16,128]{3,0,2,1:T(8,128)(2,1)S(1)}, u32[]{:S(2)}, u32[]{:S(2)}) collective-permute-start(bf16[32,8,16,128]{3,0,2,1:T(8,128)(2,1)S(1)} %copy.31), channel_id=1, source_target_pairs={{0,16},{16,32},{32,48},{48,64},{64,80},{80,96},{96,112},{112,128},... | collective-permute-start | bytes 3145736 | tf_op jit(solution)/shard_map/ppermute | solution.py:17
  11.4 1.9 collective-permute-start.1
  13.3 25.0 %collective-permute-done = bf16[32,8,16,128]{3,0,2,1:T(8,128)(2,1)S(1)} collective-permute-done((bf16[32,8,16,128]{3,0,2,1:T(8,128)(2,1)S(1)}, bf16[32,8,16,128]{3,0,2,1:T(8,128)(2,1)S(1)}, u32[]{:S(2)}, u32[]{:S(2)}) %collective-permute-start) | collective-permute-done | bytes 1048608 | tf_op jit(solution)/shard_map/ppermute | solution.py:17
  38.3 2.0 pad_slice_fusion.51
  41.1 2.0 constant_dynamic-update-slice_fusion
  43.2 2.2 fusion.227
  45.3 22.2 %collective-permute-start.3 = (bf16[32,24,8,128]{3,0,2,1:T(8,128)(2,1)}, bf16[32,24,8,128]{3,0,2,1:T(8,128)(2,1)}, u32[]{:S(2)}, u32[]{:S(2)}) collective-permute-start(bf16[32,24,8,128]{3,0,2,1:T(8,128)(2,1)} %get-tuple-element.22), channel_id=1, source_target_pairs={{1,0},{2,1},{3,2},{4,3},{5,4},{6,5},{7,6},{8,7},{9,8},{10,9},{11,1... | collective-permute-start | bytes 4718600 | tf_op jit(solution)/shard_map/ppermute | solution.py:19
  67.5 2.1 collective-permute-start.2
  70.6 2.4 pad_slice_fusion.45
  77.5 24.7 %collective-permute-done.3 = bf16[32,24,8,128]{3,0,2,1:T(8,128)(2,1)} collective-permute-done((bf16[32,24,8,128]{3,0,2,1:T(8,128)(2,1)}, bf16[32,24,8,128]{3,0,2,1:T(8,128)(2,1)}, u32[]{:S(2)}, u32[]{:S(2)}) %collective-permute-start.3) | collective-permute-done | bytes 1572896 | tf_op jit(solution)/shard_map/ppermute | solution.py:19
  102.2 33.2 %collective-permute-done.2 = bf16[32,24,8,128]{3,0,2,1:T(8,128)(2,1)} collective-permute-done((bf16[32,24,8,128]{3,0,2,1:T(8,128)(2,1)}, bf16[32,24,8,128]{3,0,2,1:T(8,128)(2,1)}, u32[]{:S(2)}, u32[]{:S(2)}) %collective-permute-start.2) | collective-permute-done | bytes 1572896 | tf_op jit(solution)/shard_map/ppermute | solution.py:17
  135.4 2.8 pad_maximum_fusion.14
  138.2 1.6 pad_slice_fusion.37
  139.8 1.6 pad_slice_fusion.43
  141.4 1.6 pad_slice_fusion.49
  146.7 1.6 fusion.162
  148.3 3.7 %collective-permute-start.5 = (bf16[32,8,16,128]{3,0,2,1:T(8,128)(2,1)S(1)}, bf16[32,8,16,128]{3,0,2,1:T(8,128)(2,1)S(1)}, u32[]{:S(2)}, u32[]{:S(2)}) collective-permute-start(bf16[32,8,16,128]{3,0,2,1:T(8,128)(2,1)S(1)} %fusion.162), channel_id=1, source_target_pairs={{16,0},{32,16},{48,32},{64,48},{80,64},{96,80},{112,96},{128,112},... | collective-permute-start | bytes 3145736 | tf_op jit(solution)/shard_map/ppermute | solution.py:19
  152.0 5.8 %collective-permute-start.4 = (bf16[32,8,16,128]{3,0,2,1:T(8,128)(2,1)S(1)}, bf16[32,8,16,128]{3,0,2,1:T(8,128)(2,1)S(1)}, u32[]{:S(2)}, u32[]{:S(2)}) collective-permute-start(bf16[32,8,16,128]{3,0,2,1:T(8,128)(2,1)S(1)} %fusion.162), channel_id=1, source_target_pairs={{0,16},{16,32},{32,48},{48,64},{64,80},{80,96},{96,112},{112,128},... | collective-permute-start | bytes 3145736 | tf_op jit(solution)/shard_map/ppermute | solution.py:17
  157.7 42.8 %collective-permute-done.5 = bf16[32,8,16,128]{3,0,2,1:T(8,128)(2,1)S(1)} collective-permute-done((bf16[32,8,16,128]{3,0,2,1:T(8,128)(2,1)S(1)}, bf16[32,8,16,128]{3,0,2,1:T(8,128)(2,1)S(1)}, u32[]{:S(2)}, u32[]{:S(2)}) %collective-permute-start.5) | collective-permute-done | bytes 1048608 | tf_op jit(solution)/shard_map/ppermute | solution.py:19
  200.9 2.2 fusion.226
  203.1 1.9 collective-permute-start.6
  205.0 6.3 %collective-permute-start.7 = (bf16[32,24,8,128]{3,0,2,1:T(8,128)(2,1)}, bf16[32,24,8,128]{3,0,2,1:T(8,128)(2,1)}, u32[]{:S(2)}, u32[]{:S(2)}) collective-permute-start(bf16[32,24,8,128]{3,0,2,1:T(8,128)(2,1)} %get-tuple-element.17), channel_id=1, source_target_pairs={{1,0},{2,1},{3,2},{4,3},{5,4},{6,5},{7,6},{8,7},{9,8},{10,9},{11,1... | collective-permute-start | bytes 4718600 | tf_op jit(solution)/shard_map/ppermute | solution.py:19
  213.0 31.1 %collective-permute-done.6 = bf16[32,24,8,128]{3,0,2,1:T(8,128)(2,1)} collective-permute-done((bf16[32,24,8,128]{3,0,2,1:T(8,128)(2,1)}, bf16[32,24,8,128]{3,0,2,1:T(8,128)(2,1)}, u32[]{:S(2)}, u32[]{:S(2)}) %collective-permute-start.6) | collective-permute-done | bytes 1572896 | tf_op jit(solution)/shard_map/ppermute | solution.py:17
  244.1 3.0 pad_maximum_fusion.13
  248.9 28.1 %collective-permute-done.7 = bf16[32,24,8,128]{3,0,2,1:T(8,128)(2,1)} collective-permute-done((bf16[32,24,8,128]{3,0,2,1:T(8,128)(2,1)}, bf16[32,24,8,128]{3,0,2,1:T(8,128)(2,1)}, u32[]{:S(2)}, u32[]{:S(2)}) %collective-permute-start.7) | collective-permute-done | bytes 1572896 | tf_op jit(solution)/shard_map/ppermute | solution.py:19
  277.0 5.2 %pad_maximum_fusion.4 = (bf16[32,8,16,128]{3,0,2,1:T(8,128)(2,1)S(1)}, bf16[32,8,16,128]{3,0,2,1:T(8,128)(2,1)S(1)}, bf16[32,8,16,128]{3,0,2,1:T(8,128)(2,1)S(1)...) fusion(bf16[32,24,8,128]{3,0,2,1:T(8,128)(2,1)} %collective-per, ...), kind=kLoop, calls=%fused_computation.223 | loop fusion | flops 12582912 | bytes 14155776 | tf_op jit(solution)/shard_map/concatenate | solution.py:15
  291.5 7.0 %collective-permute-start.8 = (bf16[32,1,16,128]{3,0,2,1:T(8,128)(2,1)S(1)}, bf16[32,1,16,128]{3,0,2,1:T(8,128)(2,1)S(1)}, u32[]{:S(2)}, u32[]{:S(2)}) collective-permute-start(bf16[32,1,16,128]{3,0,2,1:T(8,128)(2,1)S(1)} %get-tuple-element.54), channel_id=1, source_target_pairs={{0,16},{16,32},{32,48},{48,64},{64,80},{80,96},{96,112},{112,128},... | collective-permute-start | bytes 393224 | tf_op jit(solution)/shard_map/ppermute | solution.py:17
  298.5 1.9 collective-permute-start.9
  301.2 8.8 %collective-permute-done.9 = bf16[32,1,16,128]{3,0,2,1:T(8,128)(2,1)S(1)} collective-permute-done((bf16[32,1,16,128]{3,0,2,1:T(8,128)(2,1)S(1)}, bf16[32,1,16,128]{3,0,2,1:T(8,128)(2,1)S(1)}, u32[]{:S(2)}, u32[]{:S(2)}) %collective-permute-start.9) | collective-permute-done | bytes 131104 | tf_op jit(solution)/shard_map/ppermute | solution.py:19
  310.1 3.5 %collective-permute-start.10 = (bf16[32,10,1,128]{3,0,2,1:T(8,128)(2,1)S(1)}, bf16[32,10,1,128]{3,0,2,1:T(8,128)(2,1)S(1)}, u32[]{:S(2)}, u32[]{:S(2)}) collective-permute-start(bf16[32,10,1,128]{3,0,2,1:T(8,128)(2,1)S(1)} %get-tuple-element.32), channel_id=1, source_target_pairs={{0,1},{1,2},{2,3},{3,4},{4,5},{5,6},{6,7},{7,8},{8,9},{9,10},{10,1... | collective-permute-start | bytes 245768 | tf_op jit(solution)/shard_map/ppermute | solution.py:17
  313.6 4.7 %collective-permute-start.11 = (bf16[32,10,1,128]{3,0,2,1:T(8,128)(2,1)S(1)}, bf16[32,10,1,128]{3,0,2,1:T(8,128)(2,1)S(1)}, u32[]{:S(2)}, u32[]{:S(2)}) collective-permute-start(bf16[32,10,1,128]{3,0,2,1:T(8,128)(2,1)S(1)} %get-tuple-element.33), channel_id=1, source_target_pairs={{1,0},{2,1},{3,2},{4,3},{5,4},{6,5},{7,6},{8,7},{9,8},{10,9},{11,1... | collective-permute-start | bytes 245768 | tf_op jit(solution)/shard_map/ppermute | solution.py:19
  (134 shorter events, 36.2 us)
Async XLA Ops:
  0.0 40.4 %copy-start.2 = (bf16[32,8,16,128]{3,2,1,0:T(8,128)(2,1)S(1)}, bf16[32,8,16,128]{3,2,1,0:T(8,128)(2,1)}, u32[]{:S(2)}) copy-start(bf16[32,8,16,128]{3,2,1,0:T(8,128)(2,1)} %param.7) | copy-start | bytes 3145732
  2.0 39.1 %copy-start = (bf16[32,8,16,128]{3,0,2,1:T(8,128)(2,1)}, bf16[32,8,16,128]{3,0,2,1:T(8,128)(2,1)S(1)}, u32[]{:S(2)}) copy-start(bf16[32,8,16,128]{3,0,2,1:T(8,128)(2,1)S(1)} %copy.31) | copy-start | bytes 3145732
  2.0 36.3 %collective-permute-start = (bf16[32,8,16,128]{3,0,2,1:T(8,128)(2,1)S(1)}, bf16[32,8,16,128]{3,0,2,1:T(8,128)(2,1)S(1)}, u32[]{:S(2)}, u32[]{:S(2)}) collective-permute-start(bf16[32,8,16,128]{3,0,2,1:T(8,128)(2,1)S(1)} %copy.31), channel_id=1, source_target_pairs={{0,16},{16,32},{32,48},{48,64},{64,80},{80,96},{96,112},{112,128},... | collective-permute-start | bytes 3145736 | tf_op jit(solution)/shard_map/ppermute | solution.py:17
  11.4 29.7 %collective-permute-start.1 = (bf16[32,8,16,128]{3,0,2,1:T(8,128)(2,1)S(1)}, bf16[32,8,16,128]{3,0,2,1:T(8,128)(2,1)S(1)}, u32[]{:S(2)}, u32[]{:S(2)}) collective-permute-start(bf16[32,8,16,128]{3,0,2,1:T(8,128)(2,1)S(1)} %copy.31), channel_id=1, source_target_pairs={{16,0},{32,16},{48,32},{64,48},{80,64},{96,80},{112,96},{128,112},... | collective-permute-start | bytes 3145736 | tf_op jit(solution)/shard_map/ppermute | solution.py:19
  38.3 2.8 copy-start.5
  41.1 4.2 %copy-start.3 = (bf16[32,8,16,128]{3,0,2,1:T(8,128)(2,1)}, bf16[32,8,16,128]{3,0,2,1:T(8,128)(2,1)S(1)}, u32[]{:S(2)}) copy-start(bf16[32,8,16,128]{3,0,2,1:T(8,128)(2,1)S(1)} %collective-permute-done.1) | copy-start | bytes 3145732
  43.2 26.4 %copy-start.11 = (bf16[3,3,3,32,32]{4,3,2,1,0:T(8,128)(2,1)S(1)}, bf16[3,3,3,32,32]{4,3,2,1,0:T(8,128)(2,1)}, u32[]{:S(2)}) copy-start(bf16[3,3,3,32,32]{4,3,2,1,0:T(8,128)(2,1)} %param.8) | copy-start | bytes 165892
  45.3 56.8 %collective-permute-start.3 = (bf16[32,24,8,128]{3,0,2,1:T(8,128)(2,1)}, bf16[32,24,8,128]{3,0,2,1:T(8,128)(2,1)}, u32[]{:S(2)}, u32[]{:S(2)}) collective-permute-start(bf16[32,24,8,128]{3,0,2,1:T(8,128)(2,1)} %get-tuple-element.22), channel_id=1, source_target_pairs={{1,0},{2,1},{3,2},{4,3},{5,4},{6,5},{7,6},{8,7},{9,8},{10,9},{11,1... | collective-permute-start | bytes 4718600 | tf_op jit(solution)/shard_map/ppermute | solution.py:19
  67.5 67.9 %collective-permute-start.2 = (bf16[32,24,8,128]{3,0,2,1:T(8,128)(2,1)}, bf16[32,24,8,128]{3,0,2,1:T(8,128)(2,1)}, u32[]{:S(2)}, u32[]{:S(2)}) collective-permute-start(bf16[32,24,8,128]{3,0,2,1:T(8,128)(2,1)} %get-tuple-element.23), channel_id=1, source_target_pairs={{0,1},{1,2},{2,3},{3,4},{4,5},{5,6},{6,7},{7,8},{8,9},{9,10},{10,1... | collective-permute-start | bytes 4718600 | tf_op jit(solution)/shard_map/ppermute | solution.py:17
  70.6 2.4 copy-start.1
  73.0 1.2 copy-start.6
  73.0 1.5 copy-start.7
  73.0 1.8 copy-start.8
  74.9 1.2 copy-start.4
  74.9 1.5 copy-start.9
  74.9 1.9 copy-start.10
  145.9 0.7 copy-start.14
  148.3 52.3 %collective-permute-start.5 = (bf16[32,8,16,128]{3,0,2,1:T(8,128)(2,1)S(1)}, bf16[32,8,16,128]{3,0,2,1:T(8,128)(2,1)S(1)}, u32[]{:S(2)}, u32[]{:S(2)}) collective-permute-start(bf16[32,8,16,128]{3,0,2,1:T(8,128)(2,1)S(1)} %fusion.162), channel_id=1, source_target_pairs={{16,0},{32,16},{48,32},{64,48},{80,64},{96,80},{112,96},{128,112},... | collective-permute-start | bytes 3145736 | tf_op jit(solution)/shard_map/ppermute | solution.py:19
  152.0 48.6 %collective-permute-start.4 = (bf16[32,8,16,128]{3,0,2,1:T(8,128)(2,1)S(1)}, bf16[32,8,16,128]{3,0,2,1:T(8,128)(2,1)S(1)}, u32[]{:S(2)}, u32[]{:S(2)}) collective-permute-start(bf16[32,8,16,128]{3,0,2,1:T(8,128)(2,1)S(1)} %fusion.162), channel_id=1, source_target_pairs={{0,16},{16,32},{32,48},{48,64},{64,80},{80,96},{96,112},{112,128},... | collective-permute-start | bytes 3145736 | tf_op jit(solution)/shard_map/ppermute | solution.py:17
  200.9 11.0 %copy-start.12 = (bf16[3,3,3,32,32]{4,3,2,1,0:T(8,128)(2,1)S(1)}, bf16[3,3,3,32,32]{4,3,2,1,0:T(8,128)(2,1)}, u32[]{:S(2)}) copy-start(bf16[3,3,3,32,32]{4,3,2,1,0:T(8,128)(2,1)} %param.10) | copy-start | bytes 165892
  203.1 41.0 %collective-permute-start.6 = (bf16[32,24,8,128]{3,0,2,1:T(8,128)(2,1)}, bf16[32,24,8,128]{3,0,2,1:T(8,128)(2,1)}, u32[]{:S(2)}, u32[]{:S(2)}) collective-permute-start(bf16[32,24,8,128]{3,0,2,1:T(8,128)(2,1)} %get-tuple-element.18), channel_id=1, source_target_pairs={{0,1},{1,2},{2,3},{3,4},{4,5},{5,6},{6,7},{7,8},{8,9},{9,10},{10,1... | collective-permute-start | bytes 4718600 | tf_op jit(solution)/shard_map/ppermute | solution.py:17
  205.0 72.0 %collective-permute-start.7 = (bf16[32,24,8,128]{3,0,2,1:T(8,128)(2,1)}, bf16[32,24,8,128]{3,0,2,1:T(8,128)(2,1)}, u32[]{:S(2)}, u32[]{:S(2)}) collective-permute-start(bf16[32,24,8,128]{3,0,2,1:T(8,128)(2,1)} %get-tuple-element.17), channel_id=1, source_target_pairs={{1,0},{2,1},{3,2},{4,3},{5,4},{6,5},{7,6},{8,7},{9,8},{10,9},{11,1... | collective-permute-start | bytes 4718600 | tf_op jit(solution)/shard_map/ppermute | solution.py:19
  289.1 0.7 copy-start.15
  289.9 10.6 %copy-start.13 = (bf16[3,3,3,32]{3,2,1,0:T(4,128)(2,1)S(1)}, bf16[3,3,3,32]{3,2,1,0:T(4,128)(2,1)}, u32[]{:S(2)}) copy-start(bf16[3,3,3,32]{3,2,1,0:T(4,128)(2,1)} %param.12) | copy-start | bytes 5188
  291.5 9.7 %collective-permute-start.8 = (bf16[32,1,16,128]{3,0,2,1:T(8,128)(2,1)S(1)}, bf16[32,1,16,128]{3,0,2,1:T(8,128)(2,1)S(1)}, u32[]{:S(2)}, u32[]{:S(2)}) collective-permute-start(bf16[32,1,16,128]{3,0,2,1:T(8,128)(2,1)S(1)} %get-tuple-element.54), channel_id=1, source_target_pairs={{0,16},{16,32},{32,48},{48,64},{64,80},{80,96},{96,112},{112,128},... | collective-permute-start | bytes 393224 | tf_op jit(solution)/shard_map/ppermute | solution.py:17
  298.5 11.5 %collective-permute-start.9 = (bf16[32,1,16,128]{3,0,2,1:T(8,128)(2,1)S(1)}, bf16[32,1,16,128]{3,0,2,1:T(8,128)(2,1)S(1)}, u32[]{:S(2)}, u32[]{:S(2)}) collective-permute-start(bf16[32,1,16,128]{3,0,2,1:T(8,128)(2,1)S(1)} %get-tuple-element.55), channel_id=1, source_target_pairs={{16,0},{32,16},{48,32},{64,48},{80,64},{96,80},{112,96},{128,112},... | collective-permute-start | bytes 393224 | tf_op jit(solution)/shard_map/ppermute | solution.py:19
  310.1 12.1 %collective-permute-start.10 = (bf16[32,10,1,128]{3,0,2,1:T(8,128)(2,1)S(1)}, bf16[32,10,1,128]{3,0,2,1:T(8,128)(2,1)S(1)}, u32[]{:S(2)}, u32[]{:S(2)}) collective-permute-start(bf16[32,10,1,128]{3,0,2,1:T(8,128)(2,1)S(1)} %get-tuple-element.32), channel_id=1, source_target_pairs={{0,1},{1,2},{2,3},{3,4},{4,5},{5,6},{6,7},{7,8},{8,9},{9,10},{10,1... | collective-permute-start | bytes 245768 | tf_op jit(solution)/shard_map/ppermute | solution.py:17
  313.6 8.5 %collective-permute-start.11 = (bf16[32,10,1,128]{3,0,2,1:T(8,128)(2,1)S(1)}, bf16[32,10,1,128]{3,0,2,1:T(8,128)(2,1)S(1)}, u32[]{:S(2)}, u32[]{:S(2)}) collective-permute-start(bf16[32,10,1,128]{3,0,2,1:T(8,128)(2,1)S(1)} %get-tuple-element.33), channel_id=1, source_target_pairs={{1,0},{2,1},{3,2},{4,3},{5,4},{6,5},{7,6},{8,7},{9,8},{10,9},{11,1... | collective-permute-start | bytes 245768 | tf_op jit(solution)/shard_map/ppermute | solution.py:19
where the time goes:
time: 336 us; the launch traced here: 332 us
  waiting for transfers between devices  194 us (58%)
  starting transfers between devices  70.4 us (21%)
  local copies, waits for them, and re-layouts  33.2 us (10%)
  matrix products  19.4 us (6%)
  other arithmetic  13.5 us (4%)
    ppermute x6, waiting for transfers between devices, with_halo(): lax.ppermute(head, axis, [((i + 1) % count, i) for i in range(ends)])  104 us
    ppermute x6, waiting for transfers between devices, with_halo(): lax.ppermute(tail, axis, [(i, (i + 1) % count) for i in range(ends)])  89.4 us
    ppermute x6, starting transfers between devices, with_halo(): lax.ppermute(head, axis, [((i + 1) % count, i) for i in range(ends)])  40.7 us
    ppermute x6, starting transfers between devices, with_halo(): lax.ppermute(tail, axis, [(i, (i + 1) % count) for i in range(ends)])  29.7 us
    slice x19, local copies, waits for them, and re-layouts, depth_stack(): padded[..., step * tap_spacing:step * tap_spacing + depth]  17.7 us
    dot_general x18, matrix products, conv_layer(): jnp.einsum('ok,kxyz->oxyz', matrix, stacked, preferred_element_type=jnp.f...  14.7 us
    concatenate x5, other arithmetic, with_halo(): jnp.concatenate([lax.ppermute(tail, axis, [(i, (i + 1) % count) for i in...  9.87 us
  transfers between devices with their start and end apart: 12, of which 7 were waited for; matrix products, arithmetic and copies ran while one was open for 6% of the time, Pallas kernels for 0%

commit v1 on v0

v1 whole, which is shorter than its diff:
```python
import jax
import jax.numpy as jnp
import numpy as np
from jax import lax
from jax.experimental import pallas as pl
from jax.experimental.pallas import tpu as pltpu
from jax.sharding import PartitionSpec as P

S = 8
C = 32
XQ = 16
YQ = 8
Z = 128
HALO = 3
LINE = 4
ROWS = 24
BF = jnp.bfloat16
F32 = jnp.float32


def band_kernel(w1_ref, w2_ref, o1_ref, o2_ref):
    row = lax.broadcasted_iota(jnp.int32, (C, 8 * C), 0)
    lane = lax.broadcasted_iota(jnp.int32, (C, 8 * C), 1)
    repeat = jnp.where(lax.rem(lane, C) == row, 1.0, 0.0).astype(BF)
    block = lane // C
    for w_ref, o_ref in ((w1_ref, o1_ref), (w2_ref, o2_ref)):
        for k in range(9):
            taps = [
                jnp.dot(w_ref[(a * 9 + k) * C : (a * 9 + k + 1) * C, :], repeat, preferred_element_type=F32)
                for a in range(3)
            ]
            for p in range(10):
                value = jnp.zeros((C, 8 * C), F32)
                for a in range(3):
                    if 0 <= p + a - 2 < 8:
                        value = jnp.where(block == p + a - 2, taps[a], value)
                o_ref[p * C : (p + 1) * C, k * 8 * C : (k + 1) * 8 * C] = value.astype(BF)


def z_taps(value):
    lane = lax.broadcasted_iota(jnp.int32, value.shape, 1)
    before = jnp.where(lane < S, 0.0, pltpu.roll(value, S, 1)).astype(BF)
    after = jnp.where(lane >= Z - S, 0.0, pltpu.roll(value, Z - S, 1)).astype(BF)
    return before, value.astype(BF), after


def layers_kernel(
    place_ref, own_ref, low_ref, high_ref, w1_ref, w2_ref, b1_ref, b2_ref, head_ref, out_ref, xs, hs, h2s
):
    block, dx, ext = place_ref[0], place_ref[1], place_ref[2]
    not_first = jnp.where(block > 0, 1.0, 0.0)
    not_last = jnp.where(block < 3, 1.0, 0.0)

    for y in range(-HALO, YQ + HALO):
        for h in range(2):
            part = slice(h * 8, h * 8 + 8)
            if y < 0:
                value = low_ref[y + HALO, part]
            elif y < YQ:
                value = own_ref[y // 2, part, y % 2]
            else:
                value = high_ref[y - YQ, part]
            for dz, v in enumerate(z_taps(value.reshape(8 * C, Z).astype(F32))):
                if y <= 4:
                    xs[h, y + 3, dz, :, 0:Z] = v
                if y >= 3:
                    xs[h, y - 3, dz, :, Z : 2 * Z] = v

    def layer(source, t, w_ref, b_ref):
        first = jnp.dot(
            w_ref[C : 10 * C, :], source[0, pl.ds(t, 3)].reshape(9 * 8 * C, 2 * Z), preferred_element_type=F32
        )
        second = jnp.dot(
            w_ref[0 : 9 * C, :], source[1, pl.ds(t, 3)].reshape(9 * 8 * C, 2 * Z), preferred_element_type=F32
        )
        total = jnp.concatenate(
            [first[: 7 * C], first[7 * C :] + second[: 2 * C], second[2 * C :]], axis=0
        )
        return jnp.maximum(total + b_ref[...], 0.0)

    @pl.loop(0, 6)
    def _(t):
        value = layer(xs, t, w1_ref, b1_ref)
        left = value[:, :Z] * jnp.where(t < 2, not_first, 1.0)
        right = value[:, Z:] * jnp.where(t > 3, not_last, 1.0)
        for h in range(2):
            part = slice(h * 8 * C, (h + 1) * 8 * C)
            lefts, rights = z_taps(left[part]), z_taps(right[part])
            for dz in range(3):
                hs[h, t, dz, :, 0:Z] = lefts[dz]
                hs[h, t + 1, dz, :, Z : 2 * Z] = rights[dz]

            @pl.when(t == 5)
            def _():
                for dz in range(3):
                    hs[h, 0, dz, :, Z : 2 * Z] = lefts[dz]

            @pl.when(t == 0)
            def _():
                for dz in range(3):
                    hs[h, 6, dz, :, 0:Z] = rights[dz]

    h2s[0] = jnp.zeros((YQ + 2, C, Z), BF)
    h2s[XQ + 1] = jnp.zeros((YQ + 2, C, Z), BF)

    @pl.loop(0, 5)
    def _(t):
        value = layer(hs, t, w2_ref, b2_ref)
        left = value[:, :Z] * jnp.where(t < 1, not_first, 1.0)
        right = value[:, Z:] * jnp.where(t > 3, not_last, 1.0)
        h2s[1 : XQ + 1, t] = left.astype(BF).reshape(XQ, C, Z)
        h2s[1 : XQ + 1, t + 5] = right.astype(BF).reshape(XQ, C, Z)

    lane = lax.broadcasted_iota(jnp.int32, (ROWS, Z), 1)
    for l in range(0, LINE, 2):

        @pl.loop(0, XQ // 2)
        def _(pair):
            halves = ([], [])
            for sub in range(2):
                x = pair * 2 + sub + 1
                columns = []
                for k in (l, l + 1):
                    y = 2 * k + 1
                    columns.append(
                        jnp.concatenate(
                            [h2s[x + dx * e, at] for e in range(2) for at in (y, y + 1, y + ext)], axis=0
                        )
                    )
                sums = jnp.dot(
                    head_ref[...], jnp.concatenate(columns, axis=1), preferred_element_type=F32
                )
                for k in range(2):
                    part = sums[:, k * Z : (k + 1) * Z]
                    before = jnp.where(lane < 1, 0.0, pltpu.roll(part[:ROWS], 1, 1))
                    after = jnp.where(lane >= Z - 1, 0.0, pltpu.roll(part[2 * ROWS :], Z - 1, 1))
                    halves[k].append(part[ROWS : 2 * ROWS] + before + after)
            for k in range(2):
                at = pl.multiple_of(((l + k) * XQ + pair * 2) * ROWS, 16)
                out_ref[pl.ds(at, 2 * ROWS), :] = jnp.concatenate(halves[k], axis=0).astype(BF)


def finish_kernel(back_ref, pick_ref, b_ref, out_ref):
    totals = [None] * S
    for r in range(S):
        sums = jnp.dot(
            pick_ref[...], back_ref[r * S * ROWS : (r + 1) * S * ROWS, :], preferred_element_type=F32
        )
        for a in range(3):
            to = (r - (a - 1)) % S
            part = sums[a * 16 : (a + 1) * 16]
            totals[to] = part if totals[to] is None else totals[to] + part
    for x in range(S):
        out_ref[x] = 1.0 / (1.0 + jnp.exp(-(totals[x] + b_ref[0])))


def pick_matrix():
    pick = np.zeros((3, 2, S, S, ROWS), np.float32)
    for a in range(3):
        for e in range(2):
            for y in range(S):
                for b in range(3):
                    pick[a, e, y, (y + b - 1) % S, e * 9 + a * 3 + b] = 1.0
    return pick.reshape(3 * 2 * S, S * ROWS).astype(jnp.bfloat16)


def head_matrix(w_last, r, s):
    a = jnp.arange(3)[None, :, None]
    b = jnp.arange(3)[None, None, :]
    e = jnp.arange(2)[:, None, None]
    x_from = jnp.where(((a == 2) & (r == 0)) | ((a == 0) & (r == S - 1)), 1, 0)
    up = (b == 2) & (s == 0)
    down = (b == 0) & (s == S - 1)
    y_from = jnp.where(up, e + 1, jnp.where(down, jnp.where(e == 0, 2, 0), e))
    source = x_from * 3 + y_from
    mask = (source[..., None] == jnp.arange(6)).astype(BF)
    weight = jnp.transpose(w_last, (2, 0, 1, 3))
    full = mask[None, :, :, :, :, None] * weight[:, None, :, :, None, :]
    full = full.reshape(3, 18, 6 * C)
    return jnp.pad(full, ((0, 0), (0, ROWS - 18), (0, 0))).reshape(3 * ROWS, 6 * C)


VMEM = pl.BlockSpec(memory_space=pltpu.VMEM)
SMEM = pl.BlockSpec(memory_space=pltpu.SMEM)


def make_body(groups, steps):
    axes = ("inline", "crosslin")

    def swap(value):
        return lax.all_to_all(value, axes, 0, 0, tiled=True, axis_index_groups=groups)

    def body(features, w1, b1, w2, b2, w_last, b_last):
        j = lax.axis_index("crosslin")
        block = j // LINE
        k = lax.rem(j, LINE) * XQ + lax.axis_index("inline")
        r, s = k // S, lax.rem(k, S)

        send = features.reshape(C, S, 2, S, Z).transpose(1, 3, 2, 0, 4).reshape(S * S, 2 * C, Z)
        own = swap(send).reshape(LINE, XQ, 2, C, Z)
        first = jnp.stack([own[0, :, 0], own[0, :, 1], own[1, :, 0]])
        last = jnp.stack([own[2, :, 1], own[3, :, 0], own[3, :, 1]])
        ends = steps - LINE
        high = lax.ppermute(first, "crosslin", [(i + LINE, i) for i in range(ends)])
        low = lax.ppermute(last, "crosslin", [(i, i + LINE) for i in range(ends)])

        band1, band2 = pl.pallas_call(
            band_kernel,
            out_shape=[jax.ShapeDtypeStruct((10 * C, 9 * 8 * C), BF)] * 2,
            in_specs=[VMEM] * 2,
            out_specs=[VMEM] * 2,
            cost_estimate=pl.CostEstimate(flops=60000000, bytes_accessed=3200000, transcendentals=0),
        )(w1.reshape(27 * C, C), w2.reshape(27 * C, C))

        dx = jnp.where(r == 0, 1, jnp.where(r == S - 1, -1, 0))
        ext = jnp.where(s == S - 1, -1, 2)
        place = jnp.stack([block, dx, ext, 0]).astype(jnp.int32)
        bias1 = jnp.tile(b1, XQ)[:, None]
        bias2 = jnp.tile(b2, XQ)[:, None]
        parts = pl.pallas_call(
            layers_kernel,
            out_shape=jax.ShapeDtypeStruct((S * S * ROWS, Z), BF),
            in_specs=[SMEM] + [VMEM] * 8,
            out_specs=VMEM,
            scratch_shapes=[
                pltpu.VMEM((2, 8, 3, 8 * C, 2 * Z), BF),
                pltpu.VMEM((2, 7, 3, 8 * C, 2 * Z), BF),
                pltpu.VMEM((XQ + 2, YQ + 2, C, Z), BF),
            ],
            compiler_params=pltpu.CompilerParams(vmem_limit_bytes=48 << 20),
            cost_estimate=pl.CostEstimate(flops=8000000000, bytes_accessed=6000000, transcendentals=0),
        )(place, own, low, high, band1, band2, bias1, bias2, head_matrix(w_last, r, s))

        back = swap(parts.reshape(S * S, ROWS, Z)).reshape(S * S * ROWS, Z)
        return pl.pallas_call(
            finish_kernel,
            out_shape=jax.ShapeDtypeStruct((S, 2 * S, Z), F32),
            in_specs=[VMEM, VMEM, SMEM],
            out_specs=VMEM,
        )(back, jnp.asarray(pick_matrix()), b_last)

    return body


def solution(mesh):
    rows, steps = mesh.shape["inline"], mesh.shape["crosslin"]
    groups = [
        [i * steps + x * LINE + l for l in range(LINE) for i in range(rows)] for x in range(steps // LINE)
    ]
    return jax.shard_map(
        make_body(groups, steps),
        mesh=mesh,
        in_specs=(P(None, "inline", "crosslin", None), P(), P(), P(), P(), P(), P()),
        out_specs=P("inline", "crosslin", None),
        check_vma=False,
    )
```

time: 336 us -> 105 us (0.31)
  the two profiles are of different devices: /device:TPU:11 before, /device:TPU:1 now
where the time goes in v1:
time: 105 us; the launch traced here: 104 us
  waiting for transfers between devices  49.6 us (47%)
  starting transfers between devices  23.5 us (22%)
  Pallas kernels  22.3 us (21%)
  local copies, waits for them, and re-layouts  7.32 us (7%)
    all_to_all x2, waiting for transfers between devices, swap(): lax.all_to_all(value, axes, 0, 0, tiled=True, axis_index_groups=groups)  45.6 us
    all_to_all x2, starting transfers between devices, swap(): lax.all_to_all(value, axes, 0, 0, tiled=True, axis_index_groups=groups)  18.2 us
    pallas_call x1, Pallas kernels, body(): pl.pallas_call(layers_kernel, out_shape=jax.ShapeDtypeStruct((S * S * ROW...  17.3 us
    ppermute x1, starting transfers between devices, body(): low = lax.ppermute(last, 'crosslin', [(i, i + LINE) for i in range(ends)])  4.01 us
    unnamed x12, local copies, waits for them, and re-layouts  3.5 us
    pallas_call x1, Pallas kernels, body(): pl.pallas_call(band_kernel, out_shape=[jax.ShapeDtypeStruct((10 * C, 9 *...  3.08 us
    transpose x1, local copies, waits for them, and re-layouts, body(): features.reshape(C, S, 2, S, Z).transpose(1, 3, 2, 0, 4)  2.88 us
    ppermute x1, waiting for transfers between devices, body(): high = lax.ppermute(first, 'crosslin', [(i + LINE, i) for i in range(ends)])  2.22 us
  transfers between devices with their start and end apart: 4, of which 4 were waited for; matrix products, arithmetic and copies ran while one was open for 1% of the time, Pallas kernels for 3%

profile of v1, /device:TPU:1, one launch (start us, length us, event | category | flops | bytes accessed | tf_op | source)
XLA Modules:
  0.0 104.0 jit_solution(3333295849834613509)
XLA Ops:
  0.0 2.9 %copy.20 = bf16[8,8,2,32,128]{4,3,2,1,0:T(8,128)(2,1)} copy(bf16[8,8,2,32,128]{4,1,2,0,3:T(8,128)(2,1)} %bitcast.42) | data formatting | bytes 2097152 | tf_op jit(solution)/shard_map/transpose | solution.py:199
  2.9 13.2 %all-to-all-start = ((bf16[64,64,128]{2,1,0:T(8,128)(2,1)}), bf16[64,64,128]{2,1,0:T(8,128)(2,1)S(1)}, u32[]{:S(2)}, u32[]{:S(2)}) async-start(bf16[64,64,128]{2,1,0:T(8,128)(2,1)} %bitcast.5), calls=%async_computation | async-start | bytes 2097152 | tf_op jit(solution)/shard_map/all_to_all | solution.py:191
  16.1 0.1 select_select_fusion
  16.2 0.1 broadcast_add_fusion
  16.3 29.9 %all-to-all-done = bf16[64,64,128]{2,1,0:T(8,128)(2,1)S(1)} async-done(((bf16[64,64,128]{2,1,0:T(8,128)(2,1)}), bf16[64,64,128]{2,1,0:T(8,128)(2,1)S(1)}, u32[]{:S(2)}, u32[]{:S(2)}) %all-to-all-start) | async-done | bytes 1048608 | tf_op jit(solution)/shard_map/all_to_all | solution.py:191
  46.2 0.0 copy-start.3
  46.2 0.0 copy-start.4
  46.2 0.1 slice_bitcast_fusion.2
  46.3 0.0 copy-start.5
  46.3 1.3 %collective-permute-start.1 = (bf16[3,16,32,128]{3,2,1,0:T(8,128)(2,1)S(1)}, bf16[3,16,32,128]{3,2,1,0:T(8,128)(2,1)S(1)}, u32[]{:S(2)}, u32[]{:S(2)}) collective-permute-start(bf16[3,16,32,128]{3,2,1,0:T(8,128)(2,1)S(1)} %pad_maximum_fusion.1), channel_id=1, source_target_pairs={{4,0},{5,1},{6,2},{7,3},{8,4},{9,5},{10,6},{11,7},{12,8},{13,9},{1... | collective-permute-start | bytes 1179656 | tf_op jit(solution)/shard_map/ppermute | solution.py:204
  47.7 4.0 %collective-permute-start = (bf16[3,16,32,128]{3,2,1,0:T(8,128)(2,1)S(1)}, bf16[3,16,32,128]{3,2,1,0:T(8,128)(2,1)S(1)}, u32[]{:S(2)}, u32[]{:S(2)}) collective-permute-start(bf16[3,16,32,128]{3,2,1,0:T(8,128)(2,1)S(1)} %pad_maximum_fusion), channel_id=1, source_target_pairs={{0,4},{1,5},{2,6},{3,7},{4,8},{5,9},{6,10},{7,11},{8,12},{9,13},{1... | collective-permute-start | bytes 1179656 | tf_op jit(solution)/shard_map/ppermute | solution.py:205
  51.7 0.1 fusion
  51.8 0.1 mul.33
  51.9 0.1 mul.34
  52.0 0.0 copy-done.3
  52.0 0.1 mul.37
  52.2 0.0 copy-done.4
  52.2 0.3 broadcast_in_dim_tile.8.b1_ref
  52.5 0.0 copy-done.5
  52.5 0.3 broadcast_in_dim_tile.9.b2_ref
  52.8 3.1 %shard_map.82 = (bf16[320,2304]{1,0:T(8,128)(2,1)}, bf16[320,2304]{1,0:T(8,128)(2,1)}) custom-call(bf16[864,32]{1,0:T(8,128)(2,1)} %bitcast.43, bf16[864,32]{1,0:T(8,128)(2,1)} %bitcast.44), custom_call_target="tpu_custom_call" | custom-call | flops 60000000 | bytes 3200000 | tf_op jit(solution)/shard_map/pallas_call | solution.py:207
  55.9 0.1 pad_add_fusion.place_ref
  55.9 2.2 %collective-permute-done.1.high_ref = bf16[3,16,32,128]{3,2,1,0:T(8,128)(2,1)S(1)} collective-permute-done((bf16[3,16,32,128]{3,2,1,0:T(8,128)(2,1)S(1)}, bf16[3,16,32,128]{3,2,1,0:T(8,128)(2,1)S(1)}, u32[]{:S(2)}, u32[]{:S(2)}) %collective-permute-start.1) | collective-permute-done | bytes 393248 | tf_op jit(solution)/shard_map/ppermute | solution.py:204
  58.2 1.8 %collective-permute-done.low_ref = bf16[3,16,32,128]{3,2,1,0:T(8,128)(2,1)S(1)} collective-permute-done((bf16[3,16,32,128]{3,2,1,0:T(8,128)(2,1)S(1)}, bf16[3,16,32,128]{3,2,1,0:T(8,128)(2,1)S(1)}, u32[]{:S(2)}, u32[]{:S(2)}) %collective-permute-start) | collective-permute-done | bytes 393248 | tf_op jit(solution)/shard_map/ppermute | solution.py:205
  60.0 0.0 copy-start
  60.0 1.4 %copy-done = bf16[320,2304]{1,0:T(8,128)(2,1)S(1)} copy-done((bf16[320,2304]{1,0:T(8,128)(2,1)S(1)}, bf16[320,2304]{1,0:T(8,128)(2,1)}, u32[]{:S(2)}) %copy-start) | copy-done | bytes 1474584
  61.3 1.4 %copy-done.1 = bf16[320,2304]{1,0:T(8,128)(2,1)S(1)} copy-done((bf16[320,2304]{1,0:T(8,128)(2,1)S(1)}, bf16[320,2304]{1,0:T(8,128)(2,1)}, u32[]{:S(2)}) %copy-start.1) | copy-done | bytes 1474584
  62.7 17.3 %shard_map.83 = bf16[1536,128]{1,0:T(8,128)(2,1)} custom-call(s32[4]{0:T(128)S(1)} %pad_add_fusion.place_ref, bf16[4,16,2,32,128]{4,3,2,1,0:T(8,128)(2,1)S(1)} %bitcast.39, bf16[3,16,32,128]{3,2,1,0:T(8,128)(2,1)S(1)} %collective-permute-done.low_ref, bf16[3,16,32,128]{3,2,1,0:T(8,128)(2,1)S(1)} %collective-permute-done.1.high_ref, ...), custom_call_target="tpu_custom_call" | custom-call | flops 8000000000 | bytes 6000000 | tf_op jit(solution)/shard_map/pallas_call | solution.py:220
  80.0 5.0 %all-to-all-start.1 = ((bf16[64,24,128]{2,1,0:T(8,128)(2,1)}), bf16[64,24,128]{2,1,0:T(8,128)(2,1)S(1)}, u32[]{:S(2)}, u32[]{:S(2)}) async-start(bf16[64,24,128]{2,1,0:T(8,128)(2,1)} %bitcast.17), calls=%async_computation.1 | async-start | bytes 786432 | tf_op jit(solution)/shard_map/all_to_all | solution.py:191
  85.7 15.7 %all-to-all-done.1 = bf16[64,24,128]{2,1,0:T(8,128)(2,1)S(1)} async-done(((bf16[64,24,128]{2,1,0:T(8,128)(2,1)}), bf16[64,24,128]{2,1,0:T(8,128)(2,1)S(1)}, u32[]{:S(2)}, u32[]{:S(2)}) %all-to-all-start.1) | async-done | bytes 393248 | tf_op jit(solution)/shard_map/all_to_all | solution.py:191
  101.4 0.7 copy-done.2
  102.1 1.9 %shard_map.84 = f32[8,16,128]{2,1,0:T(8,128)} custom-call(bf16[1536,128]{1,0:T(8,128)(2,1)} %bitcast.41, bf16[48,192]{1,0:T(8,128)(2,1)} %constant.53.clone.pick_ref, f32[1]{0:T(128)S(6)} %copy.36.b_ref), custom_call_target="tpu_custom_call" | custom-call | tf_op jit(solution)/shard_map/pallas_call | solution.py:235
  (13 shorter events, 0.2 us)
Async XLA Ops:
  2.9 43.3 %all-to-all-start = ((bf16[64,64,128]{2,1,0:T(8,128)(2,1)}), bf16[64,64,128]{2,1,0:T(8,128)(2,1)S(1)}, u32[]{:S(2)}, u32[]{:S(2)}) async-start(bf16[64,64,128]{2,1,0:T(8,128)(2,1)} %bitcast.5), calls=%async_computation | async-start | bytes 2097152 | tf_op jit(solution)/shard_map/all_to_all | solution.py:191
  46.2 5.8 %copy-start.3 = (bf16[3,3,3,32]{3,2,1,0:T(4,128)(2,1)S(1)}, bf16[3,3,3,32]{3,2,1,0:T(4,128)(2,1)}, u32[]{:S(2)}) copy-start(bf16[3,3,3,32]{3,2,1,0:T(4,128)(2,1)} %param.13) | copy-start | bytes 5188
  46.2 6.0 %copy-start.4 = (f32[32]{0:T(128)S(1)}, f32[32]{0:T(128)}, u32[]{:S(2)}) copy-start(f32[32]{0:T(128)} %param.10) | copy-start | bytes 388
  46.3 6.2 %copy-start.5 = (f32[32]{0:T(128)S(1)}, f32[32]{0:T(128)}, u32[]{:S(2)}) copy-start(f32[32]{0:T(128)} %param.12) | copy-start | bytes 388
  46.3 11.8 %collective-permute-start.1 = (bf16[3,16,32,128]{3,2,1,0:T(8,128)(2,1)S(1)}, bf16[3,16,32,128]{3,2,1,0:T(8,128)(2,1)S(1)}, u32[]{:S(2)}, u32[]{:S(2)}) collective-permute-start(bf16[3,16,32,128]{3,2,1,0:T(8,128)(2,1)S(1)} %pad_maximum_fusion.1), channel_id=1, source_target_pairs={{4,0},{5,1},{6,2},{7,3},{8,4},{9,5},{10,6},{11,7},{12,8},{13,9},{1... | collective-permute-start | bytes 1179656 | tf_op jit(solution)/shard_map/ppermute | solution.py:204
  47.7 12.3 %collective-permute-start = (bf16[3,16,32,128]{3,2,1,0:T(8,128)(2,1)S(1)}, bf16[3,16,32,128]{3,2,1,0:T(8,128)(2,1)S(1)}, u32[]{:S(2)}, u32[]{:S(2)}) collective-permute-start(bf16[3,16,32,128]{3,2,1,0:T(8,128)(2,1)S(1)} %pad_maximum_fusion), channel_id=1, source_target_pairs={{0,4},{1,5},{2,6},{3,7},{4,8},{5,9},{6,10},{7,11},{8,12},{9,13},{1... | collective-permute-start | bytes 1179656 | tf_op jit(solution)/shard_map/ppermute | solution.py:205
  60.0 1.4 %copy-start = (bf16[320,2304]{1,0:T(8,128)(2,1)S(1)}, bf16[320,2304]{1,0:T(8,128)(2,1)}, u32[]{:S(2)}) copy-start(bf16[320,2304]{1,0:T(8,128)(2,1)} %get-tuple-element.7.w1_ref) | copy-start | bytes 4423684
  61.3 1.4 %copy-start.1 = (bf16[320,2304]{1,0:T(8,128)(2,1)S(1)}, bf16[320,2304]{1,0:T(8,128)(2,1)}, u32[]{:S(2)}) copy-start(bf16[320,2304]{1,0:T(8,128)(2,1)} %get-tuple-element.8.w2_ref) | copy-start | bytes 4423684
  80.0 21.4 %all-to-all-start.1 = ((bf16[64,24,128]{2,1,0:T(8,128)(2,1)}), bf16[64,24,128]{2,1,0:T(8,128)(2,1)S(1)}, u32[]{:S(2)}, u32[]{:S(2)}) async-start(bf16[64,24,128]{2,1,0:T(8,128)(2,1)} %bitcast.17), calls=%async_computation.1 | async-start | bytes 786432 | tf_op jit(solution)/shard_map/all_to_all | solution.py:191
  101.4 0.7 copy-start.2

commit v2 on v1

v2 whole, which is shorter than its diff:
```python
import jax
import jax.numpy as jnp
import numpy as np
from jax import lax
from jax.experimental import pallas as pl
from jax.experimental.pallas import tpu as pltpu
from jax.sharding import PartitionSpec as P

S = 8
C = 32
XQ = 16
YQ = 8
Z = 128
HALO = 3
LINE = 4
HALF = 8 * C
ROWS = 24
BF = jnp.bfloat16
F32 = jnp.float32


def band_kernel(w1_ref, w2_ref, o1_ref, o2_ref):
    row = lax.broadcasted_iota(jnp.int32, (C, HALF), 0)
    lane = lax.broadcasted_iota(jnp.int32, (C, HALF), 1)
    repeat = jnp.where(lax.rem(lane, C) == row, 1.0, 0.0).astype(BF)
    block = lane // C
    for w_ref, o_ref in ((w1_ref, o1_ref), (w2_ref, o2_ref)):
        for dy in range(3):
            for dz in range(3):
                taps = [
                    jnp.dot(
                        w_ref[((a * 3 + dy) * 3 + dz) * C : ((a * 3 + dy) * 3 + dz + 1) * C, :],
                        repeat,
                        preferred_element_type=F32,
                    )
                    for a in range(3)
                ]
                for p in range(10):
                    value = jnp.zeros((C, HALF), F32)
                    for a in range(3):
                        if 0 <= p + a - 2 < 8:
                            value = jnp.where(block == p + a - 2, taps[a], value)
                    at = (dz * 10 + p) * C
                    o_ref[at : at + C, dy * HALF : (dy + 1) * HALF] = value.astype(BF)


def layer_pair(fetch, first, second, w_ref, b_ref, sums, keep):
    for h in range(2):
        taps = jnp.concatenate(
            [w_ref[(dz * 10 + 1 - h) * C : (dz * 10 + 10 - h) * C, :] for dz in range(3)], axis=0
        )
        window = jnp.concatenate(
            [
                jnp.concatenate([fetch(first + dy, h), fetch(second + dy, h)], axis=1)
                for dy in (-1, 0, 1)
            ],
            axis=0,
        )
        sums[h] = jnp.dot(taps, window, preferred_element_type=F32)
    lane = lax.broadcasted_iota(jnp.int32, (C, Z), 1)
    bias = b_ref[...]
    for x in range(XQ):
        for side, y in enumerate((first, second)):
            lanes = slice(side * Z, (side + 1) * Z)
            parts = []
            for dz in range(3):
                part = None
                if x <= 8:
                    part = sums[0, (dz * 9 + x) * C : (dz * 9 + x + 1) * C, lanes]
                if x >= 7:
                    other = sums[1, (dz * 9 + x - 7) * C : (dz * 9 + x - 6) * C, lanes]
                    part = other if part is None else part + other
                parts.append(part)
            total = parts[1] + jnp.where(lane < S, 0.0, pltpu.roll(parts[0], S, 1))
            total = total + jnp.where(lane >= Z - S, 0.0, pltpu.roll(parts[2], Z - S, 1))
            keep(x, y, jnp.maximum(total + bias, 0.0))


def inner_kernel(own_ref, w1_ref, w2_ref, b1_ref, b2_ref, one_ref, two_ref, sums):
    def features(y, h):
        return own_ref[y // 2, h * 8 : h * 8 + 8, y % 2].reshape(HALF, Z)

    def hidden(y, h):
        return one_ref[y - 1, h * HALF : (h + 1) * HALF, :]

    def keep_one(x, y, value):
        one_ref[y - 1, x * C : (x + 1) * C, :] = value.astype(BF)

    def keep_two(x, y, value):
        two_ref[x, y - 2] = value.astype(BF)

    for y in range(1, 4):
        layer_pair(features, y, y + 3, w1_ref, b1_ref, sums, keep_one)
    for y in range(2, 4):
        layer_pair(hidden, y, y + 2, w2_ref, b2_ref, sums, keep_two)


def outer_kernel(
    place_ref, own_ref, low_ref, high_ref, one_ref, two_ref, w1_ref, w2_ref, b1_ref, b2_ref, head_ref, out_ref,
    edge, h2s, sums,
):
    block, dx, ext = place_ref[0], place_ref[1], place_ref[2]
    not_first = jnp.where(block > 0, 1.0, 0.0)
    not_last = jnp.where(block < 3, 1.0, 0.0)

    def inside(y, value):
        return value * not_first if y < 0 else value * not_last if y >= YQ else value

    def features(y, h):
        part = slice(h * 8, h * 8 + 8)
        if y < 0:
            value = low_ref[y + HALO, part]
        elif y < YQ:
            value = own_ref[y // 2, part, y % 2]
        else:
            value = high_ref[y - YQ, part]
        return value.reshape(HALF, Z)

    def hidden(y, h):
        part = slice(h * HALF, (h + 1) * HALF)
        if 1 <= y <= 6:
            return one_ref[y - 1, part, :]
        return edge[y + 2 if y < 1 else y - 4, part, :]

    def keep_one(x, y, value):
        edge[y + 2 if y < 1 else y - 4, x * C : (x + 1) * C, :] = inside(y, value).astype(BF)

    def keep_two(x, y, value):
        h2s[x + 1, y + 1] = inside(y, value).astype(BF)

    for y in range(-2, 1):
        layer_pair(features, y, y + 9, w1_ref, b1_ref, sums, keep_one)
    h2s[0] = jnp.zeros((YQ + 2, C, Z), BF)
    h2s[XQ + 1] = jnp.zeros((YQ + 2, C, Z), BF)
    for x in range(XQ):
        h2s[x + 1, 3:7] = two_ref[x]
    for y in range(-1, 2):
        layer_pair(hidden, y, y + 7, w2_ref, b2_ref, sums, keep_two)

    lane = lax.broadcasted_iota(jnp.int32, (ROWS, Z), 1)
    for l in range(0, LINE, 2):
        for pair in range(0, XQ, 2):
            halves = ([], [])
            for x in (pair + 1, pair + 2):
                columns = []
                for k in (l, l + 1):
                    y = 2 * k + 1
                    columns.append(
                        jnp.concatenate(
                            [h2s[at_x, at] for at_x in (x, x + dx) for at in (y, y + 1, y + ext)], axis=0
                        )
                    )
                both = jnp.dot(head_ref[...], jnp.concatenate(columns, axis=1), preferred_element_type=F32)
                for k in range(2):
                    part = both[:, k * Z : (k + 1) * Z]
                    before = jnp.where(lane < 1, 0.0, pltpu.roll(part[:ROWS], 1, 1))
                    after = jnp.where(lane >= Z - 1, 0.0, pltpu.roll(part[2 * ROWS :], Z - 1, 1))
                    halves[k].append(part[ROWS : 2 * ROWS] + before + after)
            for k in range(2):
                at = ((l + k) * XQ + pair) * ROWS
                out_ref[at : at + 2 * ROWS, :] = jnp.concatenate(halves[k], axis=0).astype(BF)


def finish_kernel(back_ref, pick_ref, b_ref, out_ref):
    totals = [None] * S
    for r in range(S):
        sums = jnp.dot(
            pick_ref[...], back_ref[r * S * ROWS : (r + 1) * S * ROWS, :], preferred_element_type=F32
        )
        for a in range(3):
            to = (r - (a - 1)) % S
            part = sums[a * 16 : (a + 1) * 16]
            totals[to] = part if totals[to] is None else totals[to] + part
    for x in range(S):
        out_ref[x] = 1.0 / (1.0 + jnp.exp(-(totals[x] + b_ref[0])))


def pick_matrix():
    pick = np.zeros((3, 2, S, S, ROWS), np.float32)
    for a in range(3):
        for e in range(2):
            for y in range(S):
                for b in range(3):
                    pick[a, e, y, (y + b - 1) % S, e * 9 + a * 3 + b] = 1.0
    return pick.reshape(3 * 2 * S, S * ROWS).astype(jnp.bfloat16)


def head_matrix(w_last, r, s):
    a = jnp.arange(3)[None, :, None]
    b = jnp.arange(3)[None, None, :]
    e = jnp.arange(2)[:, None, None]
    x_from = jnp.where(((a == 2) & (r == 0)) | ((a == 0) & (r == S - 1)), 1, 0)
    up = (b == 2) & (s == 0)
    down = (b == 0) & (s == S - 1)
    y_from = jnp.where(up, e + 1, jnp.where(down, jnp.where(e == 0, 2, 0), e))
    source = x_from * 3 + y_from
    mask = (source[..., None] == jnp.arange(6)).astype(BF)
    weight = jnp.transpose(w_last, (2, 0, 1, 3))
    full = mask[None, :, :, :, :, None] * weight[:, None, :, :, None, :]
    full = full.reshape(3, 18, 6 * C)
    return jnp.pad(full, ((0, 0), (0, ROWS - 18), (0, 0))).reshape(3 * ROWS, 6 * C)


VMEM = pl.BlockSpec(memory_space=pltpu.VMEM)
SMEM = pl.BlockSpec(memory_space=pltpu.SMEM)


def make_body(groups, steps):
    axes = ("inline", "crosslin")

    def swap(value):
        return lax.all_to_all(value, axes, 0, 0, tiled=True, axis_index_groups=groups)

    def body(features, w1, b1, w2, b2, w_last, b_last):
        j = lax.axis_index("crosslin")
        block = j // LINE
        k = lax.rem(j, LINE) * XQ + lax.axis_index("inline")
        r, s = k // S, lax.rem(k, S)

        send = features.reshape(C, S, 2, S, Z).transpose(1, 3, 2, 0, 4).reshape(S * S, 2 * C, Z)
        own = swap(send)
        band1, band2 = pl.pallas_call(
            band_kernel,
            out_shape=[jax.ShapeDtypeStruct((30 * C, 3 * HALF), BF)] * 2,
            in_specs=[VMEM] * 2,
            out_specs=[VMEM] * 2,
            compiler_params=pltpu.CompilerParams(vmem_limit_bytes=16 << 20),
            cost_estimate=pl.CostEstimate(flops=60000000, bytes_accessed=3200000, transcendentals=0),
        )(w1.reshape(27 * C, C), w2.reshape(27 * C, C))
        dx = jnp.where(r == 0, 1, jnp.where(r == S - 1, -1, 0))
        ext = jnp.where(s == S - 1, -1, 2)
        place = jnp.stack([block, dx, ext, 0]).astype(jnp.int32)
        head = head_matrix(w_last, r, s)
        bias1, bias2 = (jnp.broadcast_to(b[:, None], (C, Z)) for b in (b1, b2))
        own, band1, band2, place, head, bias1, bias2 = lax.optimization_barrier(
            (own, band1, band2, place, head, bias1, bias2)
        )

        own = own.reshape(LINE, XQ, 2, C, Z)
        first = jnp.stack([own[0, :, 0], own[0, :, 1], own[1, :, 0]])
        last = jnp.stack([own[2, :, 1], own[3, :, 0], own[3, :, 1]])
        ends = steps - LINE
        high = lax.ppermute(first, "crosslin", [(i + LINE, i) for i in range(ends)])
        low = lax.ppermute(last, "crosslin", [(i, i + LINE) for i in range(ends)])

        one, two = pl.pallas_call(
            inner_kernel,
            out_shape=[jax.ShapeDtypeStruct((6, XQ * C, Z), BF), jax.ShapeDtypeStruct((XQ, 4, C, Z), BF)],
            in_specs=[VMEM] * 5,
            out_specs=[VMEM] * 2,
            scratch_shapes=[pltpu.VMEM((2, 27 * C, 2 * Z), F32)],
            compiler_params=pltpu.CompilerParams(vmem_limit_bytes=32 << 20),
            cost_estimate=pl.CostEstimate(flops=4000000000, bytes_accessed=6000000, transcendentals=0),
        )(own, band1, band2, bias1, bias2)
        parts = pl.pallas_call(
            outer_kernel,
            out_shape=jax.ShapeDtypeStruct((S * S * ROWS, Z), BF),
            in_specs=[SMEM] + [VMEM] * 10,
            out_specs=VMEM,
            scratch_shapes=[
                pltpu.VMEM((6, XQ * C, Z), BF),
                pltpu.VMEM((XQ + 2, YQ + 2, C, Z), BF),
                pltpu.VMEM((2, 27 * C, 2 * Z), F32),
            ],
            compiler_params=pltpu.CompilerParams(vmem_limit_bytes=32 << 20),
            cost_estimate=pl.CostEstimate(flops=5000000000, bytes_accessed=7000000, transcendentals=0),
        )(place, own, low, high, one, two, band1, band2, bias1, bias2, head)

        back = swap(parts.reshape(S * S, ROWS, Z)).reshape(S * S * ROWS, Z)
        return pl.pallas_call(
            finish_kernel,
            out_shape=jax.ShapeDtypeStruct((S, 2 * S, Z), F32),
            in_specs=[VMEM, VMEM, SMEM],
            out_specs=VMEM,
            compiler_params=pltpu.CompilerParams(vmem_limit_bytes=16 << 20),
        )(back, jnp.asarray(pick_matrix()), b_last)

    return body


def solution(mesh):
    rows, steps = mesh.shape["inline"], mesh.shape["crosslin"]
    groups = [
        [i * steps + x * LINE + l for l in range(LINE) for i in range(rows)] for x in range(steps // LINE)
    ]
    return jax.shard_map(
        make_body(groups, steps),
        mesh=mesh,
        in_specs=(P(None, "inline", "crosslin", None), P(), P(), P(), P(), P(), P()),
        out_specs=P("inline", "crosslin", None),
        check_vma=False,
    )
```

time: 105 us -> 92.5 us (0.88)
  Pallas kernels: 22.3 us -> 13.2 us
  local copies, waits for them, and re-layouts: 7.32 us -> 4.59 us
    pallas_call x2 -> x3, Pallas kernels: 20.4 us -> 12.3 us  [the longest x1 7.61 us: body(): pl.pallas_call(outer_kernel, out_shape=jax.ShapeDtypeStruct((S * S * ROWS...]
    all_to_all x2, waiting for transfers between devices: 45.6 us -> 43.1 us  [swap(): lax.all_to_all(value, axes, 0, 0, tiled=True, axis_index_groups=groups)]
    unnamed x12 -> x16, local copies, waits for them, and re-layouts: 3.5 us -> 1.16 us
    ppermute x1, waiting for transfers between devices: 2.22 us -> 4.18 us  [body(): high = lax.ppermute(first, 'crosslin', [(i + LINE, i) for i in range(ends)])]
  transfers between devices with their start and end apart: 4 -> 4, of which waited for: 4 -> 4; matrix products, arithmetic and copies ran while one was open for 1% -> 1% of each run, Pallas kernels for 3% -> 5%
where the time goes in v2:
time: 92.5 us; the launch traced here: 92.2 us
  waiting for transfers between devices  50 us (54%)
  starting transfers between devices  23.1 us (25%)
  Pallas kernels  13.2 us (14%)
  local copies, waits for them, and re-layouts  4.59 us (5%)
    all_to_all x2, waiting for transfers between devices, swap(): lax.all_to_all(value, axes, 0, 0, tiled=True, axis_index_groups=groups)  43.1 us
    all_to_all x2, starting transfers between devices, swap(): lax.all_to_all(value, axes, 0, 0, tiled=True, axis_index_groups=groups)  18.6 us
    pallas_call x1, Pallas kernels, body(): pl.pallas_call(outer_kernel, out_shape=jax.ShapeDtypeStruct((S * S * ROWS...  7.61 us
    ppermute x1, waiting for transfers between devices, body(): high = lax.ppermute(first, 'crosslin', [(i + LINE, i) for i in range(ends)])  4.18 us
    pallas_call x1, Pallas kernels, body(): pl.pallas_call(inner_kernel, out_shape=[jax.ShapeDtypeStruct((6, XQ * C,...  3.93 us
    ppermute x1, starting transfers between devices, body(): low = lax.ppermute(last, 'crosslin', [(i, i + LINE) for i in range(ends)])  3.27 us
    transpose x1, local copies, waits for them, and re-layouts, body(): features.reshape(C, S, 2, S, Z).transpose(1, 3, 2, 0, 4)  2.89 us
    ppermute x1, waiting for transfers between devices, body(): low = lax.ppermute(last, 'crosslin', [(i, i + LINE) for i in range(ends)])  2.68 us
  transfers between devices with their start and end apart: 4, of which 4 were waited for; matrix products, arithmetic and copies ran while one was open for 1% of the time, Pallas kernels for 5%

profile of v2, /device:TPU:1, one launch (start us, length us, event | category | flops | bytes accessed | tf_op | source)
XLA Modules:
  0.0 92.2 jit_solution(17196316437497981070)
XLA Ops:
  0.0 2.9 %copy.19 = bf16[8,8,2,32,128]{4,3,2,1,0:T(8,128)(2,1)} copy(bf16[8,8,2,32,128]{4,1,2,0,3:T(8,128)(2,1)} %bitcast.45) | data formatting | bytes 2097152 | tf_op jit(solution)/shard_map/transpose | solution.py:220
  2.9 0.0 copy-start.7
  2.9 13.3 %all-to-all-start = ((bf16[64,64,128]{2,1,0:T(8,128)(2,1)}), bf16[64,64,128]{2,1,0:T(8,128)(2,1)S(1)}, u32[]{:S(2)}, u32[]{:S(2)}) async-start(bf16[64,64,128]{2,1,0:T(8,128)(2,1)} %bitcast.2), calls=%async_computation | async-start | bytes 2097152 | tf_op jit(solution)/shard_map/all_to_all | solution.py:212
  16.3 0.0 copy-done.5
  16.3 0.1 mul.37
  16.5 0.1 select_select_fusion
  16.6 0.1 broadcast_add_fusion
  16.6 0.1 fusion
  16.7 0.1 mul.33
  16.8 0.1 mul.34
  17.0 0.0 copy-done
  17.0 0.0 copy-done.1
  17.0 0.7 shard_map.82
  17.7 0.0 copy-start.3
  17.7 1.1 %copy-done.3 = bf16[960,768]{1,0:T(8,128)(2,1)} copy-done((bf16[960,768]{1,0:T(8,128)(2,1)}, bf16[960,768]{1,0:T(8,128)(2,1)S(1)}, u32[]{:S(2)}) %copy-start.3) | copy-done | bytes 1474584
  18.9 0.1 pad_add_fusion.place_ref
  18.9 27.4 %all-to-all-done = bf16[64,64,128]{2,1,0:T(8,128)(2,1)S(1)} async-done(((bf16[64,64,128]{2,1,0:T(8,128)(2,1)}), bf16[64,64,128]{2,1,0:T(8,128)(2,1)S(1)}, u32[]{:S(2)}, u32[]{:S(2)}) %all-to-all-start) | async-done | bytes 1048608 | tf_op jit(solution)/shard_map/all_to_all | solution.py:212
  46.4 0.0 copy-done.6
  46.4 0.1 broadcast_in_dim.78.b1_ref
  46.4 0.0 copy-done.7
  46.4 0.1 broadcast_in_dim.79.b2_ref
  46.5 0.1 slice_bitcast_fusion.2
  46.6 3.3 %collective-permute-start = (bf16[3,16,32,128]{3,2,1,0:T(8,128)(2,1)S(1)}, bf16[3,16,32,128]{3,2,1,0:T(8,128)(2,1)S(1)}, u32[]{:S(2)}, u32[]{:S(2)}) collective-permute-start(bf16[3,16,32,128]{3,2,1,0:T(8,128)(2,1)S(1)} %pad_maximum_fusion), channel_id=1, source_target_pairs={{0,4},{1,5},{2,6},{3,7},{4,8},{5,9},{6,10},{7,11},{8,12},{9,13},{1... | collective-permute-start | bytes 1179656 | tf_op jit(solution)/shard_map/ppermute | solution.py:244
  50.0 1.3 %collective-permute-start.1 = (bf16[3,16,32,128]{3,2,1,0:T(8,128)(2,1)S(1)}, bf16[3,16,32,128]{3,2,1,0:T(8,128)(2,1)S(1)}, u32[]{:S(2)}, u32[]{:S(2)}) collective-permute-start(bf16[3,16,32,128]{3,2,1,0:T(8,128)(2,1)S(1)} %pad_maximum_fusion.1), channel_id=1, source_target_pairs={{4,0},{5,1},{6,2},{7,3},{8,4},{9,5},{10,6},{11,7},{12,8},{13,9},{1... | collective-permute-start | bytes 1179656 | tf_op jit(solution)/shard_map/ppermute | solution.py:243
  51.3 0.0 copy-done.4
  51.3 3.9 %shard_map.83 = (bf16[6,512,128]{2,1,0:T(8,128)(2,1)S(1)}, bf16[16,4,32,128]{3,2,1,0:T(8,128)(2,1)S(1)}) custom-call(bf16[4,16,2,32,128]{4,3,2,1,0:T(8,128)(2,1)S(1)} %bitcast.39, bf16[960,768]{1,0:T(8,128)(2,1)S(1)} %get-tuple-element.20.w1_ref, bf16[960,768]{1,0:T(8,128)(2,1)S(1)} %copy-done.4, f32[32,128]{1,0:T(8,128)S(1)} %broadcast_in_dim.78.b1_ref, ...), custom_call_target="tpu_custom_call" | custom-call | flops 4000000000 | bytes 6000000 | tf_op jit(solution)/shard_map/pallas_call | solution.py:246
  55.2 2.7 %collective-permute-done.low_ref = bf16[3,16,32,128]{3,2,1,0:T(8,128)(2,1)S(1)} collective-permute-done((bf16[3,16,32,128]{3,2,1,0:T(8,128)(2,1)S(1)}, bf16[3,16,32,128]{3,2,1,0:T(8,128)(2,1)S(1)}, u32[]{:S(2)}, u32[]{:S(2)}) %collective-permute-start) | collective-permute-done | bytes 393248 | tf_op jit(solution)/shard_map/ppermute | solution.py:244
  57.9 4.2 %collective-permute-done.1.high_ref = bf16[3,16,32,128]{3,2,1,0:T(8,128)(2,1)S(1)} collective-permute-done((bf16[3,16,32,128]{3,2,1,0:T(8,128)(2,1)S(1)}, bf16[3,16,32,128]{3,2,1,0:T(8,128)(2,1)S(1)}, u32[]{:S(2)}, u32[]{:S(2)}) %collective-permute-start.1) | collective-permute-done | bytes 393248 | tf_op jit(solution)/shard_map/ppermute | solution.py:243
  62.1 7.6 %shard_map.84 = bf16[1536,128]{1,0:T(8,128)(2,1)} custom-call(s32[4]{0:T(128)S(1)} %pad_add_fusion.place_ref, bf16[4,16,2,32,128]{4,3,2,1,0:T(8,128)(2,1)S(1)} %bitcast.40, bf16[3,16,32,128]{3,2,1,0:T(8,128)(2,1)S(1)} %collective-permute-done.low_ref, bf16[3,16,32,128]{3,2,1,0:T(8,128)(2,1)S(1)} %collective-permute-done.1.high_ref, ...), custom_call_target="tpu_custom_call" | custom-call | flops 5000000000 | bytes 7000000 | tf_op jit(solution)/shard_map/pallas_call | solution.py:255
  69.7 5.3 %all-to-all-start.1 = ((bf16[64,24,128]{2,1,0:T(8,128)(2,1)}), bf16[64,24,128]{2,1,0:T(8,128)(2,1)S(1)}, u32[]{:S(2)}, u32[]{:S(2)}) async-start(bf16[64,24,128]{2,1,0:T(8,128)(2,1)} %bitcast.17), calls=%async_computation.1 | async-start | bytes 786432 | tf_op jit(solution)/shard_map/all_to_all | solution.py:212
  75.6 15.7 %all-to-all-done.1 = bf16[64,24,128]{2,1,0:T(8,128)(2,1)S(1)} async-done(((bf16[64,24,128]{2,1,0:T(8,128)(2,1)}), bf16[64,24,128]{2,1,0:T(8,128)(2,1)S(1)}, u32[]{:S(2)}, u32[]{:S(2)}) %all-to-all-start.1) | async-done | bytes 393248 | tf_op jit(solution)/shard_map/all_to_all | solution.py:212
  91.3 0.9 shard_map.85
  (16 shorter events, 0.2 us)
Async XLA Ops:
  2.9 13.4 %copy-start.5 = (bf16[3,3,3,32]{3,2,1,0:T(4,128)(2,1)S(1)}, bf16[3,3,3,32]{3,2,1,0:T(4,128)(2,1)}, u32[]{:S(2)}) copy-start(bf16[3,3,3,32]{3,2,1,0:T(4,128)(2,1)} %param.13) | copy-start | bytes 5188
  2.9 14.1 %copy-start = (bf16[3,3,3,32,32]{4,3,2,1,0:T(8,128)(2,1)S(1)}, bf16[3,3,3,32,32]{4,3,2,1,0:T(8,128)(2,1)}, u32[]{:S(2)}) copy-start(bf16[3,3,3,32,32]{4,3,2,1,0:T(8,128)(2,1)} %param.9) | copy-start | bytes 165892
  2.9 14.1 %copy-start.1 = (bf16[3,3,3,32,32]{4,3,2,1,0:T(8,128)(2,1)S(1)}, bf16[3,3,3,32,32]{4,3,2,1,0:T(8,128)(2,1)}, u32[]{:S(2)}) copy-start(bf16[3,3,3,32,32]{4,3,2,1,0:T(8,128)(2,1)} %param.11) | copy-start | bytes 165892
  2.9 43.5 %copy-start.6 = (f32[32]{0:T(128)S(1)}, f32[32]{0:T(128)}, u32[]{:S(2)}) copy-start(f32[32]{0:T(128)} %param.10) | copy-start | bytes 388
  2.9 43.5 %copy-start.7 = (f32[32]{0:T(128)S(1)}, f32[32]{0:T(128)}, u32[]{:S(2)}) copy-start(f32[32]{0:T(128)} %param.12) | copy-start | bytes 388
  2.9 43.4 %all-to-all-start = ((bf16[64,64,128]{2,1,0:T(8,128)(2,1)}), bf16[64,64,128]{2,1,0:T(8,128)(2,1)S(1)}, u32[]{:S(2)}, u32[]{:S(2)}) async-start(bf16[64,64,128]{2,1,0:T(8,128)(2,1)} %bitcast.2), calls=%async_computation | async-start | bytes 2097152 | tf_op jit(solution)/shard_map/all_to_all | solution.py:212
  17.7 1.1 %copy-start.3 = (bf16[960,768]{1,0:T(8,128)(2,1)}, bf16[960,768]{1,0:T(8,128)(2,1)S(1)}, u32[]{:S(2)}) copy-start(bf16[960,768]{1,0:T(8,128)(2,1)S(1)} %get-tuple-element.21.w2_ref) | copy-start | bytes 4423684
  46.5 4.8 %copy-start.4 = (bf16[960,768]{1,0:T(8,128)(2,1)S(1)}, bf16[960,768]{1,0:T(8,128)(2,1)}, u32[]{:S(2)}) copy-start(bf16[960,768]{1,0:T(8,128)(2,1)} %copy-done.3) | copy-start | bytes 4423684
  46.6 11.3 %collective-permute-start = (bf16[3,16,32,128]{3,2,1,0:T(8,128)(2,1)S(1)}, bf16[3,16,32,128]{3,2,1,0:T(8,128)(2,1)S(1)}, u32[]{:S(2)}, u32[]{:S(2)}) collective-permute-start(bf16[3,16,32,128]{3,2,1,0:T(8,128)(2,1)S(1)} %pad_maximum_fusion), channel_id=1, source_target_pairs={{0,4},{1,5},{2,6},{3,7},{4,8},{5,9},{6,10},{7,11},{8,12},{9,13},{1... | collective-permute-start | bytes 1179656 | tf_op jit(solution)/shard_map/ppermute | solution.py:244
  50.0 12.1 %collective-permute-start.1 = (bf16[3,16,32,128]{3,2,1,0:T(8,128)(2,1)S(1)}, bf16[3,16,32,128]{3,2,1,0:T(8,128)(2,1)S(1)}, u32[]{:S(2)}, u32[]{:S(2)}) collective-permute-start(bf16[3,16,32,128]{3,2,1,0:T(8,128)(2,1)S(1)} %pad_maximum_fusion.1), channel_id=1, source_target_pairs={{4,0},{5,1},{6,2},{7,3},{8,4},{9,5},{10,6},{11,7},{12,8},{13,9},{1... | collective-permute-start | bytes 1179656 | tf_op jit(solution)/shard_map/ppermute | solution.py:243
  62.1 29.2 %copy-start.2 = (bf16[48,192]{1,0:T(8,128)(2,1)S(1)}, bf16[48,192]{1,0:T(8,128)(2,1)}, u32[]{:S(2)}) copy-start(bf16[48,192]{1,0:T(8,128)(2,1)} %constant.53.clone.pick_ref) | copy-start | bytes 55300
  69.7 21.6 %all-to-all-start.1 = ((bf16[64,24,128]{2,1,0:T(8,128)(2,1)}), bf16[64,24,128]{2,1,0:T(8,128)(2,1)S(1)}, u32[]{:S(2)}, u32[]{:S(2)}) async-start(bf16[64,24,128]{2,1,0:T(8,128)(2,1)} %bitcast.17), calls=%async_computation.1 | async-start | bytes 786432 | tf_op jit(solution)/shard_map/all_to_all | solution.py:212

commit v3 on v2

--- a/solution.py
+++ b/solution.py
@@ -11,7 +11,6 @@
 XQ = 16
 YQ = 8
 Z = 128
-HALO = 3
 LINE = 4
 HALF = 8 * C
 ROWS = 24
@@ -44,23 +43,20 @@
                     o_ref[at : at + C, dy * HALF : (dy + 1) * HALF] = value.astype(BF)
 
 
-def layer_pair(fetch, first, second, w_ref, b_ref, sums, keep):
+def layer_at(windows, w_ref, b_ref, sums, keep):
+    wide = len(windows) * Z
     for h in range(2):
         taps = jnp.concatenate(
             [w_ref[(dz * 10 + 1 - h) * C : (dz * 10 + 10 - h) * C, :] for dz in range(3)], axis=0
         )
         window = jnp.concatenate(
-            [
-                jnp.concatenate([fetch(first + dy, h), fetch(second + dy, h)], axis=1)
-                for dy in (-1, 0, 1)
-            ],
-            axis=0,
+            [jnp.concatenate([at(dy, h) for at in windows], axis=1) for dy in (-1, 0, 1)], axis=0
         )
-        sums[h] = jnp.dot(taps, window, preferred_element_type=F32)
+        sums[h, :, 0:wide] = jnp.dot(taps, window, preferred_element_type=F32)
     lane = lax.broadcasted_iota(jnp.int32, (C, Z), 1)
     bias = b_ref[...]
     for x in range(XQ):
-        for side, y in enumerate((first, second)):
+        for side in range(len(windows)):
             lanes = slice(side * Z, (side + 1) * Z)
             parts = []
             for dz in range(3):
@@ -73,7 +69,15 @@
                 parts.append(part)
             total = parts[1] + jnp.where(lane < S, 0.0, pltpu.roll(parts[0], S, 1))
             total = total + jnp.where(lane >= Z - S, 0.0, pltpu.roll(parts[2], Z - S, 1))
-            keep(x, y, jnp.maximum(total + bias, 0.0))
+            keep(x, side, jnp.maximum(total + bias, 0.0))
+
+
+def layer_pair(fetch, first, second, w_ref, b_ref, sums, keep):
+    pair = (first, second)
+    layer_at(
+        [lambda dy, h, y=y: fetch(y + dy, h) for y in pair],
+        w_ref, b_ref, sums, lambda x, side, value: keep(x, pair[side], value),
+    )
 
 
 def inner_kernel(own_ref, w1_ref, w2_ref, b1_ref, b2_ref, one_ref, two_ref, sums):
@@ -96,24 +100,30 @@
 
 
 def outer_kernel(
-    place_ref, own_ref, low_ref, high_ref, one_ref, two_ref, w1_ref, w2_ref, b1_ref, b2_ref, head_ref, out_ref,
-    edge, h2s, sums,
+    place_ref, own_ref, low_ref, high_ref, far_ref, one_ref, two_ref, w1_ref, w2_ref, b1_ref, b2_ref, head_ref,
+    out_ref, ends, edge, h2s, sums,
 ):
-    block, dx, ext = place_ref[0], place_ref[1], place_ref[2]
+    block, dx, ext, start = place_ref[0], place_ref[1], place_ref[2], place_ref[3]
     not_first = jnp.where(block > 0, 1.0, 0.0)
     not_last = jnp.where(block < 3, 1.0, 0.0)
+    ninth = jnp.where(start == 0, not_first, not_last)
 
     def inside(y, value):
         return value * not_first if y < 0 else value * not_last if y >= YQ else value
 
+    def slot(y):
+        return y + 3 if y < 0 else y - 5
+
+    for x in range(XQ):
+        ends[0, x] = far_ref[x]
+        ends[5, x] = far_ref[x]
+        for y in range(2):
+            ends[1 + y, x] = low_ref[x, y]
+            ends[3 + y, x] = high_ref[x, y]
+
     def features(y, h):
         part = slice(h * 8, h * 8 + 8)
-        if y < 0:
-            value = low_ref[y + HALO, part]
-        elif y < YQ:
-            value = own_ref[y // 2, part, y % 2]
-        else:
-            value = high_ref[y - YQ, part]
+        value = own_ref[y // 2, part, y % 2] if 0 <= y < YQ else ends[slot(y), part]
         return value.reshape(HALF, Z)
 
     def hidden(y, h):
@@ -126,16 +136,30 @@
         edge[y + 2 if y < 1 else y - 4, x * C : (x + 1) * C, :] = inside(y, value).astype(BF)
 
     def keep_two(x, y, value):
-        h2s[x + 1, y + 1] = inside(y, value).astype(BF)
-
-    for y in range(-2, 1):
-        layer_pair(features, y, y + 9, w1_ref, b1_ref, sums, keep_one)
+        h2s[x + 1, y + 1] = value.astype(BF)
+
+    def keep_one_ninth(x, side, value):
+        edge[jnp.where(start == 0, 0, 5), x * C : (x + 1) * C, :] = (value * ninth).astype(BF)
+
+    def keep_two_ninth(x, side, value):
+        h2s[x + 1, jnp.where(start == 0, 0, 9)] = (value * ninth).astype(BF)
+
+    for y in (-1, 0):
+        layer_pair(features, y, y + 8, w1_ref, b1_ref, sums, keep_one)
+    layer_at(
+        [lambda dy, h: ends[start + 1 + dy, h * 8 : h * 8 + 8].reshape(HALF, Z)],
+        w1_ref, b1_ref, sums, keep_one_ninth,
+    )
     h2s[0] = jnp.zeros((YQ + 2, C, Z), BF)
     h2s[XQ + 1] = jnp.zeros((YQ + 2, C, Z), BF)
     for x in range(XQ):
         h2s[x + 1, 3:7] = two_ref[x]
-    for y in range(-1, 2):
-        layer_pair(hidden, y, y + 7, w2_ref, b2_ref, sums, keep_two)
+    for y in (0, 1):
+        layer_pair(hidden, y, y + 6, w2_ref, b2_ref, sums, keep_two)
+    layer_at(
+        [lambda dy, h: edge[start + 1 + dy, h * HALF : (h + 1) * HALF, :]],
+        w2_ref, b2_ref, sums, keep_two_ninth,
+    )
 
     lane = lax.broadcasted_iota(jnp.int32, (ROWS, Z), 1)
     for l in range(0, LINE, 2):
@@ -205,7 +229,7 @@
 SMEM = pl.BlockSpec(memory_space=pltpu.SMEM)
 
 
-def make_body(groups, steps):
+def make_body(groups, far_pairs, steps):
     axes = ("inline", "crosslin")
 
     def swap(value):
@@ -229,7 +253,7 @@
         )(w1.reshape(27 * C, C), w2.reshape(27 * C, C))
         dx = jnp.where(r == 0, 1, jnp.where(r == S - 1, -1, 0))
         ext = jnp.where(s == S - 1, -1, 2)
-        place = jnp.stack([block, dx, ext, 0]).astype(jnp.int32)
+        place = jnp.stack([block, dx, ext, jnp.where(s == S - 1, 0, 3)]).astype(jnp.int32)
         head = head_matrix(w_last, r, s)
         bias1, bias2 = (jnp.broadcast_to(b[:, None], (C, Z)) for b in (b1, b2))
         own, band1, band2, place, head, bias1, bias2 = lax.optimization_barrier(
@@ -237,11 +261,10 @@
         )
 
         own = own.reshape(LINE, XQ, 2, C, Z)
-        first = jnp.stack([own[0, :, 0], own[0, :, 1], own[1, :, 0]])
-        last = jnp.stack([own[2, :, 1], own[3, :, 0], own[3, :, 1]])
-        ends = steps - LINE
-        high = lax.ppermute(first, "crosslin", [(i + LINE, i) for i in range(ends)])
-        low = lax.ppermute(last, "crosslin", [(i, i + LINE) for i in range(ends)])
+        far = jnp.where(s == S - 1, own[2, :, 1], own[1, :, 0])
+        high = lax.ppermute(own[0], "crosslin", [(i + LINE, i) for i in range(steps - LINE)])
+        low = lax.ppermute(own[3], "crosslin", [(i, i + LINE) for i in range(steps - LINE)])
+        far = lax.ppermute(far, axes, far_pairs)
 
         one, two = pl.pallas_call(
             inner_kernel,
@@ -255,16 +278,17 @@
         parts = pl.pallas_call(
             outer_kernel,
             out_shape=jax.ShapeDtypeStruct((S * S * ROWS, Z), BF),
-            in_specs=[SMEM] + [VMEM] * 10,
+            in_specs=[SMEM] + [VMEM] * 11,
             out_specs=VMEM,
             scratch_shapes=[
+                pltpu.VMEM((6, XQ, C, Z), BF),
                 pltpu.VMEM((6, XQ * C, Z), BF),
                 pltpu.VMEM((XQ + 2, YQ + 2, C, Z), BF),
                 pltpu.VMEM((2, 27 * C, 2 * Z), F32),
             ],
             compiler_params=pltpu.CompilerParams(vmem_limit_bytes=32 << 20),
             cost_estimate=pl.CostEstimate(flops=5000000000, bytes_accessed=7000000, transcendentals=0),
-        )(place, own, low, high, one, two, band1, band2, bias1, bias2, head)
+        )(place, own, low, high, far, one, two, band1, band2, bias1, bias2, head)
 
         back = swap(parts.reshape(S * S, ROWS, Z)).reshape(S * S * ROWS, Z)
         return pl.pallas_call(
@@ -283,8 +307,16 @@
     groups = [
         [i * steps + x * LINE + l for l in range(LINE) for i in range(rows)] for x in range(steps // LINE)
     ]
+    far_pairs = []
+    for i in range(rows):
+        for at in range(steps - LINE):
+            below, above = i * steps + at, i * steps + at + LINE
+            if i % S == 0:
+                far_pairs.append((above, below))
+            if i % S == S - 1:
+                far_pairs.append((below, above))
     return jax.shard_map(
-        make_body(groups, steps),
+        make_body(groups, far_pairs, steps),
         mesh=mesh,
         in_specs=(P(None, "inline", "crosslin", None), P(), P(), P(), P(), P(), P()),
         out_specs=P("inline", "crosslin", None),

time: 92.5 us -> 89.7 us (0.970)
  waiting for transfers between devices: 50 us -> 47.3 us
    transpose x1 -> x0, local copies, waits for them, and re-layouts: 2.89 us -> none  [body(): features.reshape(C, S, 2, S, Z).transpose(1, 3, 2, 0, 4)]
    reshape x0 -> x1, local copies, waits for them, and re-layouts: none -> 2.88 us  [body(): features.reshape(C, S, 2, S, Z).transpose(1, 3, 2, 0, 4)]
    ppermute x2 -> x3, waiting for transfers between devices: 6.86 us -> 4.2 us  [the longest x1 4.19 us: body(): lax.ppermute(own[0], 'crosslin', [(i + LINE, i) for i in range(steps - LI...]
    ppermute x2 -> x3, starting transfers between devices: 4.56 us -> 5.22 us  [the longest x1 3.26 us: body(): lax.ppermute(own[3], 'crosslin', [(i, i + LINE) for i in range(steps - LI...]
  transfers between devices with their start and end apart: 4 -> 5, of which waited for: 4 -> 3; matrix products, arithmetic and copies ran while one was open for 1% -> 1% of each run, Pallas kernels for 5% -> 5%
where the time goes in v3:
time: 89.7 us; the launch traced here: 89.3 us
  waiting for transfers between devices  47.3 us (53%)
  starting transfers between devices  23.9 us (27%)
  Pallas kernels  12.3 us (14%)
  local copies, waits for them, and re-layouts  4.56 us (5%)
  between operations  0.92 us (1%)
    all_to_all x2, waiting for transfers between devices, swap(): lax.all_to_all(value, axes, 0, 0, tiled=True, axis_index_groups=groups)  43.1 us
    all_to_all x2, starting transfers between devices, swap(): lax.all_to_all(value, axes, 0, 0, tiled=True, axis_index_groups=groups)  18.7 us
    pallas_call x1, Pallas kernels, body(): pl.pallas_call(outer_kernel, out_shape=jax.ShapeDtypeStruct((S * S * ROWS...  6.71 us
    ppermute x1, waiting for transfers between devices, body(): lax.ppermute(own[0], 'crosslin', [(i + LINE, i) for i in range(steps - LI...  4.19 us
    pallas_call x1, Pallas kernels, body(): pl.pallas_call(inner_kernel, out_shape=[jax.ShapeDtypeStruct((6, XQ * C,...  3.93 us
    ppermute x1, starting transfers between devices, body(): lax.ppermute(own[3], 'crosslin', [(i, i + LINE) for i in range(steps - LI...  3.26 us
    reshape x1, local copies, waits for them, and re-layouts, body(): features.reshape(C, S, 2, S, Z).transpose(1, 3, 2, 0, 4)  2.88 us
  transfers between devices with their start and end apart: 5, of which 3 were waited for; matrix products, arithmetic and copies ran while one was open for 1% of the time, Pallas kernels for 5%

profile of v3, /device:TPU:1, one launch (start us, length us, event | category | flops | bytes accessed | tf_op | source)
XLA Modules:
  0.0 89.3 jit_solution(9777177719835840939)
XLA Ops:
  0.0 2.9 %copy.13 = bf16[32,8,2,8,128]{4,0,2,3,1:T(8,128)(2,1)} copy(bf16[32,8,2,8,128]{4,3,2,1,0:T(8,128)(2,1)} %bitcast.36) | data formatting | bytes 2097152 | tf_op jit(solution)/shard_map/reshape | solution.py:244
  2.9 0.0 copy-start.7
  2.9 13.3 %all-to-all-start = ((bf16[64,64,128]{2,1,0:T(8,128)(2,1)}), bf16[64,64,128]{2,1,0:T(8,128)(2,1)S(1)}, u32[]{:S(2)}, u32[]{:S(2)}) async-start(bf16[64,64,128]{2,1,0:T(8,128)(2,1)} %bitcast.2), calls=%async_computation | async-start | bytes 2097152 | tf_op jit(solution)/shard_map/all_to_all | solution.py:236
  16.3 0.1 select_select_fusion
  16.4 0.1 broadcast_add_fusion
  16.5 0.1 fusion.2
  16.5 0.1 mul.33
  16.6 0.1 mul.34
  16.7 0.0 copy-done.5
  16.8 0.1 mul.37
  17.0 0.0 copy-done
  17.0 0.0 copy-done.1
  17.0 0.7 shard_map.82
  17.7 0.0 copy-start.3
  17.7 1.1 %copy-done.3 = bf16[960,768]{1,0:T(8,128)(2,1)} copy-done((bf16[960,768]{1,0:T(8,128)(2,1)}, bf16[960,768]{1,0:T(8,128)(2,1)S(1)}, u32[]{:S(2)}) %copy-start.3) | copy-done | bytes 1474584
  18.8 0.1 pad_add_fusion.place_ref
  18.9 27.4 %all-to-all-done = bf16[64,64,128]{2,1,0:T(8,128)(2,1)S(1)} async-done(((bf16[64,64,128]{2,1,0:T(8,128)(2,1)}), bf16[64,64,128]{2,1,0:T(8,128)(2,1)S(1)}, u32[]{:S(2)}, u32[]{:S(2)}) %all-to-all-start) | async-done | bytes 1048608 | tf_op jit(solution)/shard_map/all_to_all | solution.py:236
  46.4 0.0 copy-done.6
  46.4 0.1 broadcast_in_dim.78.b1_ref
  46.4 0.1 broadcast_in_dim.79.b2_ref
  46.5 3.3 %collective-permute-start = (bf16[16,2,32,128]{3,2,1,0:T(8,128)(2,1)S(1)}, bf16[16,2,32,128]{3,2,1,0:T(8,128)(2,1)S(1)}, u32[]{:S(2)}, u32[]{:S(2)}) collective-permute-start(bf16[16,2,32,128]{3,2,1,0:T(8,128)(2,1)S(1)} %bitcast.38), channel_id=1, source_target_pairs={{0,4},{1,5},{2,6},{3,7},{4,8},{5,9},{6,10},{7,11},{8,12},{9,13},{1... | collective-permute-start | bytes 786440 | tf_op jit(solution)/shard_map/ppermute | solution.py:266
  49.8 1.3 %collective-permute-start.1 = (bf16[16,2,32,128]{3,2,1,0:T(8,128)(2,1)S(1)}, bf16[16,2,32,128]{3,2,1,0:T(8,128)(2,1)S(1)}, u32[]{:S(2)}, u32[]{:S(2)}) collective-permute-start(bf16[16,2,32,128]{3,2,1,0:T(8,128)(2,1)S(1)} %bitcast.37), channel_id=1, source_target_pairs={{4,0},{5,1},{6,2},{7,3},{8,4},{9,5},{10,6},{11,7},{12,8},{13,9},{1... | collective-permute-start | bytes 786440 | tf_op jit(solution)/shard_map/ppermute | solution.py:265
  51.1 0.7 collective-permute-start.2
  51.8 0.0 copy-done.4
  51.8 3.9 %shard_map.83 = (bf16[6,512,128]{2,1,0:T(8,128)(2,1)S(1)}, bf16[16,4,32,128]{3,2,1,0:T(8,128)(2,1)S(1)}) custom-call(bf16[4,16,2,32,128]{4,3,2,1,0:T(8,128)(2,1)S(1)} %bitcast.30, bf16[960,768]{1,0:T(8,128)(2,1)S(1)} %get-tuple-element.20.w1_ref, bf16[960,768]{1,0:T(8,128)(2,1)S(1)} %copy-done.4, f32[32,128]{1,0:T(8,128)S(1)} %broadcast_in_dim.78.b1_ref, ...), custom_call_target="tpu_custom_call" | custom-call | flops 4000000000 | bytes 6000000 | tf_op jit(solution)/shard_map/pallas_call | solution.py:269
  55.8 0.0 collective-permute-done.2.far_ref
  55.8 0.0 collective-permute-done.low_ref
  55.8 4.2 %collective-permute-done.1.high_ref = bf16[16,2,32,128]{3,2,1,0:T(8,128)(2,1)S(1)} collective-permute-done((bf16[16,2,32,128]{3,2,1,0:T(8,128)(2,1)S(1)}, bf16[16,2,32,128]{3,2,1,0:T(8,128)(2,1)S(1)}, u32[]{:S(2)}, u32[]{:S(2)}) %collective-permute-start.1) | collective-permute-done | bytes 262176 | tf_op jit(solution)/shard_map/ppermute | solution.py:265
  60.0 6.7 %shard_map.84 = bf16[1536,128]{1,0:T(8,128)(2,1)} custom-call(s32[4]{0:T(128)S(1)} %pad_add_fusion.place_ref, bf16[4,16,2,32,128]{4,3,2,1,0:T(8,128)(2,1)S(1)} %bitcast.31, bf16[16,2,32,128]{3,2,1,0:T(8,128)(2,1)S(1)} %collective-permute-done.low_ref, bf16[16,2,32,128]{3,2,1,0:T(8,128)(2,1)S(1)} %collective-permute-done.1.high_ref, ...), custom_call_target="tpu_custom_call" | custom-call | flops 5000000000 | bytes 7000000 | tf_op jit(solution)/shard_map/pallas_call | solution.py:278
  66.7 5.4 %all-to-all-start.1 = ((bf16[64,24,128]{2,1,0:T(8,128)(2,1)}), bf16[64,24,128]{2,1,0:T(8,128)(2,1)S(1)}, u32[]{:S(2)}, u32[]{:S(2)}) async-start(bf16[64,24,128]{2,1,0:T(8,128)(2,1)} %bitcast.15), calls=%async_computation.1 | async-start | bytes 786432 | tf_op jit(solution)/shard_map/all_to_all | solution.py:236
  72.7 15.7 %all-to-all-done.1 = bf16[64,24,128]{2,1,0:T(8,128)(2,1)S(1)} async-done(((bf16[64,24,128]{2,1,0:T(8,128)(2,1)}), bf16[64,24,128]{2,1,0:T(8,128)(2,1)S(1)}, u32[]{:S(2)}, u32[]{:S(2)}) %all-to-all-start.1) | async-done | bytes 393248 | tf_op jit(solution)/shard_map/all_to_all | solution.py:236
  88.4 0.9 %shard_map.85 = f32[8,16,128]{2,1,0:T(8,128)} custom-call(bf16[1536,128]{1,0:T(8,128)(2,1)S(1)} %bitcast.32, bf16[48,192]{1,0:T(8,128)(2,1)S(1)} %copy-done.2, f32[1]{0:T(128)S(6)} %copy.19.b_ref), custom_call_target="tpu_custom_call" | custom-call | tf_op jit(solution)/shard_map/pallas_call | solution.py:294
  (17 shorter events, 0.1 us)
Async XLA Ops:
  2.9 13.8 %copy-start.5 = (bf16[3,3,3,32]{3,2,1,0:T(4,128)(2,1)S(1)}, bf16[3,3,3,32]{3,2,1,0:T(4,128)(2,1)}, u32[]{:S(2)}) copy-start(bf16[3,3,3,32]{3,2,1,0:T(4,128)(2,1)} %param.13) | copy-start | bytes 5188
  2.9 14.1 %copy-start = (bf16[3,3,3,32,32]{4,3,2,1,0:T(8,128)(2,1)S(1)}, bf16[3,3,3,32,32]{4,3,2,1,0:T(8,128)(2,1)}, u32[]{:S(2)}) copy-start(bf16[3,3,3,32,32]{4,3,2,1,0:T(8,128)(2,1)} %param.9) | copy-start | bytes 165892
  2.9 14.1 %copy-start.1 = (bf16[3,3,3,32,32]{4,3,2,1,0:T(8,128)(2,1)S(1)}, bf16[3,3,3,32,32]{4,3,2,1,0:T(8,128)(2,1)}, u32[]{:S(2)}) copy-start(bf16[3,3,3,32,32]{4,3,2,1,0:T(8,128)(2,1)} %param.11) | copy-start | bytes 165892
  2.9 43.5 %copy-start.6 = (f32[32]{0:T(128)S(1)}, f32[32]{0:T(128)}, u32[]{:S(2)}) copy-start(f32[32]{0:T(128)} %param.10) | copy-start | bytes 388
  2.9 43.5 %copy-start.7 = (f32[32]{0:T(128)S(1)}, f32[32]{0:T(128)}, u32[]{:S(2)}) copy-start(f32[32]{0:T(128)} %param.12) | copy-start | bytes 388
  2.9 43.4 %all-to-all-start = ((bf16[64,64,128]{2,1,0:T(8,128)(2,1)}), bf16[64,64,128]{2,1,0:T(8,128)(2,1)S(1)}, u32[]{:S(2)}, u32[]{:S(2)}) async-start(bf16[64,64,128]{2,1,0:T(8,128)(2,1)} %bitcast.2), calls=%async_computation | async-start | bytes 2097152 | tf_op jit(solution)/shard_map/all_to_all | solution.py:236
  17.7 1.1 %copy-start.3 = (bf16[960,768]{1,0:T(8,128)(2,1)}, bf16[960,768]{1,0:T(8,128)(2,1)S(1)}, u32[]{:S(2)}) copy-start(bf16[960,768]{1,0:T(8,128)(2,1)S(1)} %get-tuple-element.21.w2_ref) | copy-start | bytes 4423684
  46.4 5.5 %copy-start.4 = (bf16[960,768]{1,0:T(8,128)(2,1)S(1)}, bf16[960,768]{1,0:T(8,128)(2,1)}, u32[]{:S(2)}) copy-start(bf16[960,768]{1,0:T(8,128)(2,1)} %copy-done.3) | copy-start | bytes 4423684
  46.5 9.2 %collective-permute-start = (bf16[16,2,32,128]{3,2,1,0:T(8,128)(2,1)S(1)}, bf16[16,2,32,128]{3,2,1,0:T(8,128)(2,1)S(1)}, u32[]{:S(2)}, u32[]{:S(2)}) collective-permute-start(bf16[16,2,32,128]{3,2,1,0:T(8,128)(2,1)S(1)} %bitcast.38), channel_id=1, source_target_pairs={{0,4},{1,5},{2,6},{3,7},{4,8},{5,9},{6,10},{7,11},{8,12},{9,13},{1... | collective-permute-start | bytes 786440 | tf_op jit(solution)/shard_map/ppermute | solution.py:266
  49.8 10.2 %collective-permute-start.1 = (bf16[16,2,32,128]{3,2,1,0:T(8,128)(2,1)S(1)}, bf16[16,2,32,128]{3,2,1,0:T(8,128)(2,1)S(1)}, u32[]{:S(2)}, u32[]{:S(2)}) collective-permute-start(bf16[16,2,32,128]{3,2,1,0:T(8,128)(2,1)S(1)} %bitcast.37), channel_id=1, source_target_pairs={{4,0},{5,1},{6,2},{7,3},{8,4},{9,5},{10,6},{11,7},{12,8},{13,9},{1... | collective-permute-start | bytes 786440 | tf_op jit(solution)/shard_map/ppermute | solution.py:265
  51.1 4.6 %collective-permute-start.2 = (bf16[16,32,128]{2,1,0:T(8,128)(2,1)S(1)}, bf16[16,32,128]{2,1,0:T(8,128)(2,1)S(1)}, u32[]{:S(2)}, u32[]{:S(2)}) collective-permute-start(bf16[16,32,128]{2,1,0:T(8,128)(2,1)S(1)} %fusion.1), channel_id=1, source_target_pairs={{4,0},{5,1},{6,2},{7,3},{8,4},{9,5},{10,6},{11,7},{12,8},{13,9},{1... | collective-permute-start | bytes 393224 | tf_op jit(solution)/shard_map/ppermute | solution.py:267
  60.0 28.4 %copy-start.2 = (bf16[48,192]{1,0:T(8,128)(2,1)S(1)}, bf16[48,192]{1,0:T(8,128)(2,1)}, u32[]{:S(2)}) copy-start(bf16[48,192]{1,0:T(8,128)(2,1)} %constant.52.clone.pick_ref) | copy-start | bytes 55300
  66.7 21.7 %all-to-all-start.1 = ((bf16[64,24,128]{2,1,0:T(8,128)(2,1)}), bf16[64,24,128]{2,1,0:T(8,128)(2,1)S(1)}, u32[]{:S(2)}, u32[]{:S(2)}) async-start(bf16[64,24,128]{2,1,0:T(8,128)(2,1)} %bitcast.15), calls=%async_computation.1 | async-start | bytes 786432 | tf_op jit(solution)/shard_map/all_to_all | solution.py:236

commit v4 on v3

--- a/solution.py
+++ b/solution.py
@@ -16,6 +16,25 @@
 ROWS = 24
 BF = jnp.bfloat16
 F32 = jnp.float32
+
+
+def split_kernel(in_ref, out_ref, arrived, rows, sorted_, sems, out_sems):
+    copies = [pltpu.make_async_copy(in_ref.at[:, x], arrived.at[x], sems.at[x]) for x in range(S)]
+    for copy in copies:
+        copy.start()
+    leaving = []
+    for x in range(S):
+        copies[x].wait()
+        rows[x % 2] = arrived[x].reshape(2 * S * C, Z).astype(F32)
+        for phase in range(S):
+            for step in range(2):
+                value = rows[x % 2, pl.ds(step * S + phase, C, stride=2 * S), :]
+                sorted_[x, phase, step * C : (step + 1) * C, :] = value.astype(BF)
+        leave = pltpu.make_async_copy(sorted_.at[x], out_ref.at[x * S : (x + 1) * S], out_sems.at[x])
+        leave.start()
+        leaving.append(leave)
+    for leave in leaving:
+        leave.wait()
 
 
 def band_kernel(w1_ref, w2_ref, o1_ref, o2_ref):
@@ -43,41 +62,51 @@
                     o_ref[at : at + C, dy * HALF : (dy + 1) * HALF] = value.astype(BF)
 
 
-def layer_at(windows, w_ref, b_ref, sums, keep):
-    wide = len(windows) * Z
+def finish_layer(part, steps, bias, keep):
+    lane = lax.broadcasted_iota(jnp.int32, (C, Z), 1)
+    for x in range(XQ):
+        for step in range(steps):
+            taps = []
+            for dz in range(3):
+                found = [part(h, dz, x - 7 * h, step) for h in range(2) if 0 <= x - 7 * h <= 8]
+                taps.append(found[0] if len(found) == 1 else found[0] + found[1])
+            total = taps[1] + jnp.where(lane < S, 0.0, pltpu.roll(taps[0], S, 1))
+            total = total + jnp.where(lane >= Z - S, 0.0, pltpu.roll(taps[2], Z - S, 1))
+            keep(x, step, jnp.maximum(total + bias, 0.0))
+
+
+def layer_pair(fetch, first, second, w_ref, b_ref, sums, keep):
     for h in range(2):
         taps = jnp.concatenate(
             [w_ref[(dz * 10 + 1 - h) * C : (dz * 10 + 10 - h) * C, :] for dz in range(3)], axis=0
         )
         window = jnp.concatenate(
-            [jnp.concatenate([at(dy, h) for at in windows], axis=1) for dy in (-1, 0, 1)], axis=0
+            [
+                jnp.concatenate([fetch(first + dy, h), fetch(second + dy, h)], axis=1)
+                for dy in (-1, 0, 1)
+            ],
+            axis=0,
         )
-        sums[h, :, 0:wide] = jnp.dot(taps, window, preferred_element_type=F32)
-    lane = lax.broadcasted_iota(jnp.int32, (C, Z), 1)
-    bias = b_ref[...]
-    for x in range(XQ):
-        for side in range(len(windows)):
-            lanes = slice(side * Z, (side + 1) * Z)
-            parts = []
-            for dz in range(3):
-                part = None
-                if x <= 8:
-                    part = sums[0, (dz * 9 + x) * C : (dz * 9 + x + 1) * C, lanes]
-                if x >= 7:
-                    other = sums[1, (dz * 9 + x - 7) * C : (dz * 9 + x - 6) * C, lanes]
-                    part = other if part is None else part + other
-                parts.append(part)
-            total = parts[1] + jnp.where(lane < S, 0.0, pltpu.roll(parts[0], S, 1))
-            total = total + jnp.where(lane >= Z - S, 0.0, pltpu.roll(parts[2], Z - S, 1))
-            keep(x, side, jnp.maximum(total + bias, 0.0))
-
-
-def layer_pair(fetch, first, second, w_ref, b_ref, sums, keep):
-    pair = (first, second)
-    layer_at(
-        [lambda dy, h, y=y: fetch(y + dy, h) for y in pair],
-        w_ref, b_ref, sums, lambda x, side, value: keep(x, pair[side], value),
+        sums[h] = jnp.dot(taps, window, preferred_element_type=F32)
+
+    def part(h, dz, x, step):
+        at = (dz * 9 + x) * C
+        return sums[h, at : at + C, step * Z : (step + 1) * Z]
+
+    finish_layer(part, 2, b_ref[...], lambda x, step, value: keep(x, (first, second)[step], value))
+
+
+def layer_one(fetch, w_ref, b_ref, sums, keep):
+    window = jnp.concatenate(
+        [jnp.concatenate([fetch(dy, 0), fetch(dy, 1)], axis=1) for dy in (-1, 0, 1)], axis=0
     )
+    sums[...] = jnp.dot(w_ref[...], window, preferred_element_type=F32)
+
+    def part(h, dz, x, step):
+        at = (dz * 10 + x + 1 - h) * C
+        return sums[at : at + C, h * Z : (h + 1) * Z]
+
+    finish_layer(part, 1, b_ref[...], lambda x, step, value: keep(x, value))
 
 
 def inner_kernel(own_ref, w1_ref, w2_ref, b1_ref, b2_ref, one_ref, two_ref, sums):
@@ -101,7 +130,7 @@
 
 def outer_kernel(
     place_ref, own_ref, low_ref, high_ref, far_ref, one_ref, two_ref, w1_ref, w2_ref, b1_ref, b2_ref, head_ref,
-    out_ref, ends, edge, h2s, sums,
+    out_ref, ends, edge, h2s, planes, sums, single,
 ):
     block, dx, ext, start = place_ref[0], place_ref[1], place_ref[2], place_ref[3]
     not_first = jnp.where(block > 0, 1.0, 0.0)
@@ -138,17 +167,16 @@
     def keep_two(x, y, value):
         h2s[x + 1, y + 1] = value.astype(BF)
 
-    def keep_one_ninth(x, side, value):
+    def keep_one_ninth(x, value):
         edge[jnp.where(start == 0, 0, 5), x * C : (x + 1) * C, :] = (value * ninth).astype(BF)
 
-    def keep_two_ninth(x, side, value):
+    def keep_two_ninth(x, value):
         h2s[x + 1, jnp.where(start == 0, 0, 9)] = (value * ninth).astype(BF)
 
     for y in (-1, 0):
         layer_pair(features, y, y + 8, w1_ref, b1_ref, sums, keep_one)
-    layer_at(
-        [lambda dy, h: ends[start + 1 + dy, h * 8 : h * 8 + 8].reshape(HALF, Z)],
-        w1_ref, b1_ref, sums, keep_one_ninth,
+    layer_one(
+        lambda dy, h: ends[start + 1 + dy, h * 8 : h * 8 + 8].reshape(HALF, Z), w1_ref, b1_ref, single, keep_one_ninth
     )
     h2s[0] = jnp.zeros((YQ + 2, C, Z), BF)
     h2s[XQ + 1] = jnp.zeros((YQ + 2, C, Z), BF)
@@ -156,33 +184,35 @@
         h2s[x + 1, 3:7] = two_ref[x]
     for y in (0, 1):
         layer_pair(hidden, y, y + 6, w2_ref, b2_ref, sums, keep_two)
-    layer_at(
-        [lambda dy, h: edge[start + 1 + dy, h * HALF : (h + 1) * HALF, :]],
-        w2_ref, b2_ref, sums, keep_two_ninth,
+    layer_one(
+        lambda dy, h: edge[start + 1 + dy, h * HALF : (h + 1) * HALF, :], w2_ref, b2_ref, single, keep_two_ninth
     )
 
-    lane = lax.broadcasted_iota(jnp.int32, (ROWS, Z), 1)
-    for l in range(0, LINE, 2):
-        for pair in range(0, XQ, 2):
-            halves = ([], [])
-            for x in (pair + 1, pair + 2):
-                columns = []
-                for k in (l, l + 1):
-                    y = 2 * k + 1
-                    columns.append(
-                        jnp.concatenate(
-                            [h2s[at_x, at] for at_x in (x, x + dx) for at in (y, y + 1, y + ext)], axis=0
-                        )
-                    )
-                both = jnp.dot(head_ref[...], jnp.concatenate(columns, axis=1), preferred_element_type=F32)
-                for k in range(2):
-                    part = both[:, k * Z : (k + 1) * Z]
-                    before = jnp.where(lane < 1, 0.0, pltpu.roll(part[:ROWS], 1, 1))
-                    after = jnp.where(lane >= Z - 1, 0.0, pltpu.roll(part[2 * ROWS :], Z - 1, 1))
-                    halves[k].append(part[ROWS : 2 * ROWS] + before + after)
+    lane = lax.broadcasted_iota(jnp.int32, (2 * ROWS, Z), 1)
+    planes[0] = jnp.zeros((LINE, ROWS, Z), F32)
+    planes[XQ + 1] = jnp.zeros((LINE, ROWS, Z), F32)
+    for x in range(1, XQ + 1, 2):
+        for l in range(0, LINE, 2):
+            columns = []
+            for k in (l, l + 1):
+                y = 2 * k + 1
+                columns.append(
+                    jnp.concatenate([h2s[at, step] for at in (x, x + 1) for step in (y, y + 1, y + ext)], axis=0)
+                )
+            both = jnp.dot(head_ref[...], jnp.concatenate(columns, axis=1), preferred_element_type=F32)
             for k in range(2):
-                at = ((l + k) * XQ + pair) * ROWS
-                out_ref[at : at + 2 * ROWS, :] = jnp.concatenate(halves[k], axis=0).astype(BF)
+                part = both[:, k * Z : (k + 1) * Z]
+                before = jnp.where(lane < 1, 0.0, pltpu.roll(part[: 2 * ROWS], 1, 1))
+                after = jnp.where(lane >= Z - 1, 0.0, pltpu.roll(part[4 * ROWS :], Z - 1, 1))
+                total = part[2 * ROWS : 4 * ROWS] + before + after
+                planes[x, l + k] = total[:ROWS]
+                planes[x + 1, l + k] = total[ROWS:]
+    moved = lax.rem(lax.broadcasted_iota(jnp.int32, (ROWS, Z), 0), 9) // 3 == dx + 1
+    for l in range(LINE):
+        for x in range(1, XQ + 1, 2):
+            rows = [jnp.where(moved, planes[at + dx, l], planes[at, l]) for at in (x, x + 1)]
+            at = (l * XQ + x - 1) * ROWS
+            out_ref[at : at + 2 * ROWS, :] = jnp.concatenate(rows, axis=0).astype(BF)
 
 
 def finish_kernel(back_ref, pick_ref, b_ref, out_ref):
@@ -209,20 +239,19 @@
     return pick.reshape(3 * 2 * S, S * ROWS).astype(jnp.bfloat16)
 
 
-def head_matrix(w_last, r, s):
-    a = jnp.arange(3)[None, :, None]
-    b = jnp.arange(3)[None, None, :]
-    e = jnp.arange(2)[:, None, None]
-    x_from = jnp.where(((a == 2) & (r == 0)) | ((a == 0) & (r == S - 1)), 1, 0)
+def head_matrix(w_last, s):
+    b = jnp.arange(3)[None, :]
+    e = jnp.arange(2)[:, None]
     up = (b == 2) & (s == 0)
     down = (b == 0) & (s == S - 1)
-    y_from = jnp.where(up, e + 1, jnp.where(down, jnp.where(e == 0, 2, 0), e))
-    source = x_from * 3 + y_from
-    mask = (source[..., None] == jnp.arange(6)).astype(BF)
+    source = jnp.where(up, e + 1, jnp.where(down, jnp.where(e == 0, 2, 0), e))
+    mask = (source[..., None] == jnp.arange(3)).astype(BF)
     weight = jnp.transpose(w_last, (2, 0, 1, 3))
-    full = mask[None, :, :, :, :, None] * weight[:, None, :, :, None, :]
-    full = full.reshape(3, 18, 6 * C)
-    return jnp.pad(full, ((0, 0), (0, ROWS - 18), (0, 0))).reshape(3 * ROWS, 6 * C)
+    full = mask[None, :, None, :, :, None] * weight[:, None, :, :, None, :]
+    full = jnp.pad(full.reshape(3, 18, 3 * C), ((0, 0), (0, ROWS - 18), (0, 0)))
+    zero = jnp.zeros_like(full)
+    pair = jnp.stack([jnp.concatenate([full, zero], axis=2), jnp.concatenate([zero, full], axis=2)], axis=1)
+    return pair.reshape(6 * ROWS, 6 * C)
 
 
 VMEM = pl.BlockSpec(memory_space=pltpu.VMEM)
@@ -241,7 +270,20 @@
         k = lax.rem(j, LINE) * XQ + lax.axis_index("inline")
         r, s = k // S, lax.rem(k, S)
 
-        send = features.reshape(C, S, 2, S, Z).transpose(1, 3, 2, 0, 4).reshape(S * S, 2 * C, Z)
+        send = pl.pallas_call(
+            split_kernel,
+            out_shape=jax.ShapeDtypeStruct((S * S, 2 * C, Z), BF),
+            in_specs=[pl.BlockSpec(memory_space=pltpu.HBM)],
+            out_specs=pl.BlockSpec(memory_space=pltpu.HBM),
+            scratch_shapes=[
+                pltpu.VMEM((S, C, 2 * S, Z), BF),
+                pltpu.VMEM((2, 2 * S * C, Z), F32),
+                pltpu.VMEM((S, S, 2 * C, Z), BF),
+                pltpu.SemaphoreType.DMA((S,)),
+                pltpu.SemaphoreType.DMA((S,)),
+            ],
+            compiler_params=pltpu.CompilerParams(vmem_limit_bytes=60 << 20),
+        )(features)
         own = swap(send)
         band1, band2 = pl.pallas_call(
             band_kernel,
@@ -254,7 +296,7 @@
         dx = jnp.where(r == 0, 1, jnp.where(r == S - 1, -1, 0))
         ext = jnp.where(s == S - 1, -1, 2)
         place = jnp.stack([block, dx, ext, jnp.where(s == S - 1, 0, 3)]).astype(jnp.int32)
-        head = head_matrix(w_last, r, s)
+        head = head_matrix(w_last, s)
         bias1, bias2 = (jnp.broadcast_to(b[:, None], (C, Z)) for b in (b1, b2))
         own, band1, band2, place, head, bias1, bias2 = lax.optimization_barrier(
             (own, band1, band2, place, head, bias1, bias2)
@@ -284,7 +326,9 @@
                 pltpu.VMEM((6, XQ, C, Z), BF),
                 pltpu.VMEM((6, XQ * C, Z), BF),
                 pltpu.VMEM((XQ + 2, YQ + 2, C, Z), BF),
+                pltpu.VMEM((XQ + 2, LINE, ROWS, Z), F32),
                 pltpu.VMEM((2, 27 * C, 2 * Z), F32),
+                pltpu.VMEM((30 * C, 2 * Z), F32),
             ],
             compiler_params=pltpu.CompilerParams(vmem_limit_bytes=32 << 20),
             cost_estimate=pl.CostEstimate(flops=5000000000, bytes_accessed=7000000, transcendentals=0),

time: 89.7 us -> 88.6 us (0.988)
  local copies, waits for them, and re-layouts: 4.56 us -> 1.74 us
  Pallas kernels: 12.3 us -> 14.1 us
    reshape x1 -> x0, local copies, waits for them, and re-layouts: 2.88 us -> none  [body(): features.reshape(C, S, 2, S, Z).transpose(1, 3, 2, 0, 4)]
    pallas_call x0 -> x1, Pallas kernels: none -> 2.48 us  [body(): pl.pallas_call(split_kernel, out_shape=jax.ShapeDtypeStruct((S * S, 2 * C...]
where the time goes in v4:
time: 88.6 us; the launch traced here: 88.3 us
  waiting for transfers between devices  47.3 us (53%)
  starting transfers between devices  23.9 us (27%)
  Pallas kernels  14.1 us (16%)
  local copies, waits for them, and re-layouts  1.74 us (2%)
  between operations  0.96 us (1%)
    all_to_all x2, waiting for transfers between devices, swap(): lax.all_to_all(value, axes, 0, 0, tiled=True, axis_index_groups=groups)  43.1 us
    all_to_all x2, starting transfers between devices, swap(): lax.all_to_all(value, axes, 0, 0, tiled=True, axis_index_groups=groups)  18.7 us
    pallas_call x1, Pallas kernels, body(): pl.pallas_call(outer_kernel, out_shape=jax.ShapeDtypeStruct((S * S * ROWS...  6.03 us
    ppermute x1, waiting for transfers between devices, body(): lax.ppermute(own[0], 'crosslin', [(i + LINE, i) for i in range(steps - LI...  4.18 us
    pallas_call x1, Pallas kernels, body(): pl.pallas_call(inner_kernel, out_shape=[jax.ShapeDtypeStruct((6, XQ * C,...  3.94 us
    ppermute x1, starting transfers between devices, body(): lax.ppermute(own[3], 'crosslin', [(i, i + LINE) for i in range(steps - LI...  3.26 us
    pallas_call x1, Pallas kernels, body(): pl.pallas_call(split_kernel, out_shape=jax.ShapeDtypeStruct((S * S, 2 * C...  2.48 us
  transfers between devices with their start and end apart: 5, of which 3 were waited for; matrix products, arithmetic and copies ran while one was open for 1% of the time, Pallas kernels for 5%

profile of v4, /device:TPU:1, one launch (start us, length us, event | category | flops | bytes accessed | tf_op | source)
XLA Modules:
  0.0 88.3 jit_solution(13343436008370456086)
XLA Ops:
  0.0 2.5 %shard_map.82 = bf16[64,64,128]{2,1,0:T(8,128)(2,1)} custom-call(bf16[32,8,16,128]{3,2,1,0:T(8,128)(2,1)} %in_ref.1), custom_call_target="tpu_custom_call" | custom-call | tf_op jit(solution)/shard_map/pallas_call | solution.py:273
  2.5 0.0 copy-start.5
  2.5 0.0 copy-start
  2.5 0.0 copy-start.1
  2.5 0.0 copy-start.6
  2.5 0.0 copy-start.7
  2.6 13.3 %all-to-all-start = ((bf16[64,64,128]{2,1,0:T(8,128)(2,1)}), bf16[64,64,128]{2,1,0:T(8,128)(2,1)S(1)}, u32[]{:S(2)}, u32[]{:S(2)}) async-start(bf16[64,64,128]{2,1,0:T(8,128)(2,1)} %shard_map.82), calls=%async_computation | async-start | bytes 2097152 | tf_op jit(solution)/shard_map/all_to_all | solution.py:265
  15.9 0.1 select_select_fusion
  16.0 0.1 fusion.2
  16.1 0.1 mul.24
  16.2 0.1 mul.25
  16.3 0.0 copy-done.5
  16.3 0.1 mul.28
  16.4 0.1 pad_bitcast_fusion.1
  16.6 0.7 shard_map.83
  17.4 1.1 %copy-done.3 = bf16[960,768]{1,0:T(8,128)(2,1)} copy-done((bf16[960,768]{1,0:T(8,128)(2,1)}, bf16[960,768]{1,0:T(8,128)(2,1)S(1)}, u32[]{:S(2)}) %copy-start.3) | copy-done | bytes 1474584
  18.5 0.1 pad_add_fusion.place_ref
  18.6 27.4 %all-to-all-done = bf16[64,64,128]{2,1,0:T(8,128)(2,1)S(1)} async-done(((bf16[64,64,128]{2,1,0:T(8,128)(2,1)}), bf16[64,64,128]{2,1,0:T(8,128)(2,1)S(1)}, u32[]{:S(2)}, u32[]{:S(2)}) %all-to-all-start) | async-done | bytes 1048608 | tf_op jit(solution)/shard_map/all_to_all | solution.py:265
  46.0 0.0 copy-done.6
  46.0 0.1 broadcast_in_dim.71.b1_ref
  46.1 0.1 broadcast_in_dim.72.b2_ref
  46.2 3.3 %collective-permute-start = (bf16[16,2,32,128]{3,2,1,0:T(8,128)(2,1)S(1)}, bf16[16,2,32,128]{3,2,1,0:T(8,128)(2,1)S(1)}, u32[]{:S(2)}, u32[]{:S(2)}) collective-permute-start(bf16[16,2,32,128]{3,2,1,0:T(8,128)(2,1)S(1)} %bitcast.37), channel_id=1, source_target_pairs={{0,4},{1,5},{2,6},{3,7},{4,8},{5,9},{6,10},{7,11},{8,12},{9,13},{1... | collective-permute-start | bytes 786440 | tf_op jit(solution)/shard_map/ppermute | solution.py:308
  49.5 1.3 %collective-permute-start.1 = (bf16[16,2,32,128]{3,2,1,0:T(8,128)(2,1)S(1)}, bf16[16,2,32,128]{3,2,1,0:T(8,128)(2,1)S(1)}, u32[]{:S(2)}, u32[]{:S(2)}) collective-permute-start(bf16[16,2,32,128]{3,2,1,0:T(8,128)(2,1)S(1)} %bitcast.36), channel_id=1, source_target_pairs={{4,0},{5,1},{6,2},{7,3},{8,4},{9,5},{10,6},{11,7},{12,8},{13,9},{1... | collective-permute-start | bytes 786440 | tf_op jit(solution)/shard_map/ppermute | solution.py:307
  50.8 0.7 collective-permute-start.2
  51.5 3.9 %shard_map.84 = (bf16[6,512,128]{2,1,0:T(8,128)(2,1)S(1)}, bf16[16,4,32,128]{3,2,1,0:T(8,128)(2,1)S(1)}) custom-call(bf16[4,16,2,32,128]{4,3,2,1,0:T(8,128)(2,1)S(1)} %bitcast.30, bf16[960,768]{1,0:T(8,128)(2,1)S(1)} %get-tuple-element.20.w1_ref, bf16[960,768]{1,0:T(8,128)(2,1)S(1)} %copy-done.4, f32[32,128]{1,0:T(8,128)S(1)} %broadcast_in_dim.71.b1_ref, ...), custom_call_target="tpu_custom_call" | custom-call | flops 4000000000 | bytes 6000000 | tf_op jit(solution)/shard_map/pallas_call | solution.py:311
  55.4 0.0 collective-permute-done.2.far_ref
  55.4 0.0 collective-permute-done.low_ref
  55.4 4.2 %collective-permute-done.1.high_ref = bf16[16,2,32,128]{3,2,1,0:T(8,128)(2,1)S(1)} collective-permute-done((bf16[16,2,32,128]{3,2,1,0:T(8,128)(2,1)S(1)}, bf16[16,2,32,128]{3,2,1,0:T(8,128)(2,1)S(1)}, u32[]{:S(2)}, u32[]{:S(2)}) %collective-permute-start.1) | collective-permute-done | bytes 262176 | tf_op jit(solution)/shard_map/ppermute | solution.py:307
  59.6 6.0 %shard_map.85 = bf16[1536,128]{1,0:T(8,128)(2,1)} custom-call(s32[4]{0:T(128)S(1)} %pad_add_fusion.place_ref, bf16[4,16,2,32,128]{4,3,2,1,0:T(8,128)(2,1)S(1)} %bitcast.31, bf16[16,2,32,128]{3,2,1,0:T(8,128)(2,1)S(1)} %collective-permute-done.low_ref, bf16[16,2,32,128]{3,2,1,0:T(8,128)(2,1)S(1)} %collective-permute-done.1.high_ref, ...), custom_call_target="tpu_custom_call" | custom-call | flops 5000000000 | bytes 7000000 | tf_op jit(solution)/shard_map/pallas_call | solution.py:320
  65.7 5.4 %all-to-all-start.1 = ((bf16[64,24,128]{2,1,0:T(8,128)(2,1)}), bf16[64,24,128]{2,1,0:T(8,128)(2,1)S(1)}, u32[]{:S(2)}, u32[]{:S(2)}) async-start(bf16[64,24,128]{2,1,0:T(8,128)(2,1)} %bitcast.14), calls=%async_computation.1 | async-start | bytes 786432 | tf_op jit(solution)/shard_map/all_to_all | solution.py:265
  71.7 15.7 %all-to-all-done.1 = bf16[64,24,128]{2,1,0:T(8,128)(2,1)S(1)} async-done(((bf16[64,24,128]{2,1,0:T(8,128)(2,1)}), bf16[64,24,128]{2,1,0:T(8,128)(2,1)S(1)}, u32[]{:S(2)}, u32[]{:S(2)}) %all-to-all-start.1) | async-done | bytes 393248 | tf_op jit(solution)/shard_map/all_to_all | solution.py:265
  87.4 0.9 %shard_map.86 = f32[8,16,128]{2,1,0:T(8,128)} custom-call(bf16[1536,128]{1,0:T(8,128)(2,1)S(1)} %bitcast.32, bf16[48,192]{1,0:T(8,128)(2,1)S(1)} %copy-done.2, f32[1]{0:T(128)S(6)} %copy.19.b_ref), custom_call_target="tpu_custom_call" | custom-call | tf_op jit(solution)/shard_map/pallas_call | solution.py:338
  (18 shorter events, 0.1 us)
Async XLA Ops:
  2.5 13.8 %copy-start.5 = (bf16[3,3,3,32]{3,2,1,0:T(4,128)(2,1)S(1)}, bf16[3,3,3,32]{3,2,1,0:T(4,128)(2,1)}, u32[]{:S(2)}) copy-start(bf16[3,3,3,32]{3,2,1,0:T(4,128)(2,1)} %param.13) | copy-start | bytes 5188
  2.5 14.1 %copy-start = (bf16[3,3,3,32,32]{4,3,2,1,0:T(8,128)(2,1)S(1)}, bf16[3,3,3,32,32]{4,3,2,1,0:T(8,128)(2,1)}, u32[]{:S(2)}) copy-start(bf16[3,3,3,32,32]{4,3,2,1,0:T(8,128)(2,1)} %param.9) | copy-start | bytes 165892
  2.5 14.1 %copy-start.1 = (bf16[3,3,3,32,32]{4,3,2,1,0:T(8,128)(2,1)S(1)}, bf16[3,3,3,32,32]{4,3,2,1,0:T(8,128)(2,1)}, u32[]{:S(2)}) copy-start(bf16[3,3,3,32,32]{4,3,2,1,0:T(8,128)(2,1)} %param.11) | copy-start | bytes 165892
  2.5 43.5 %copy-start.6 = (f32[32]{0:T(128)S(1)}, f32[32]{0:T(128)}, u32[]{:S(2)}) copy-start(f32[32]{0:T(128)} %param.10) | copy-start | bytes 388
  2.5 43.5 %copy-start.7 = (f32[32]{0:T(128)S(1)}, f32[32]{0:T(128)}, u32[]{:S(2)}) copy-start(f32[32]{0:T(128)} %param.12) | copy-start | bytes 388
  2.6 43.4 %all-to-all-start = ((bf16[64,64,128]{2,1,0:T(8,128)(2,1)}), bf16[64,64,128]{2,1,0:T(8,128)(2,1)S(1)}, u32[]{:S(2)}, u32[]{:S(2)}) async-start(bf16[64,64,128]{2,1,0:T(8,128)(2,1)} %shard_map.82), calls=%async_computation | async-start | bytes 2097152 | tf_op jit(solution)/shard_map/all_to_all | solution.py:265
  17.3 1.1 %copy-start.3 = (bf16[960,768]{1,0:T(8,128)(2,1)}, bf16[960,768]{1,0:T(8,128)(2,1)S(1)}, u32[]{:S(2)}) copy-start(bf16[960,768]{1,0:T(8,128)(2,1)S(1)} %get-tuple-element.21.w2_ref) | copy-start | bytes 4423684
  46.0 5.5 %copy-start.4 = (bf16[960,768]{1,0:T(8,128)(2,1)S(1)}, bf16[960,768]{1,0:T(8,128)(2,1)}, u32[]{:S(2)}) copy-start(bf16[960,768]{1,0:T(8,128)(2,1)} %copy-done.3) | copy-start | bytes 4423684
  46.2 9.2 %collective-permute-start = (bf16[16,2,32,128]{3,2,1,0:T(8,128)(2,1)S(1)}, bf16[16,2,32,128]{3,2,1,0:T(8,128)(2,1)S(1)}, u32[]{:S(2)}, u32[]{:S(2)}) collective-permute-start(bf16[16,2,32,128]{3,2,1,0:T(8,128)(2,1)S(1)} %bitcast.37), channel_id=1, source_target_pairs={{0,4},{1,5},{2,6},{3,7},{4,8},{5,9},{6,10},{7,11},{8,12},{9,13},{1... | collective-permute-start | bytes 786440 | tf_op jit(solution)/shard_map/ppermute | solution.py:308
  49.5 10.2 %collective-permute-start.1 = (bf16[16,2,32,128]{3,2,1,0:T(8,128)(2,1)S(1)}, bf16[16,2,32,128]{3,2,1,0:T(8,128)(2,1)S(1)}, u32[]{:S(2)}, u32[]{:S(2)}) collective-permute-start(bf16[16,2,32,128]{3,2,1,0:T(8,128)(2,1)S(1)} %bitcast.36), channel_id=1, source_target_pairs={{4,0},{5,1},{6,2},{7,3},{8,4},{9,5},{10,6},{11,7},{12,8},{13,9},{1... | collective-permute-start | bytes 786440 | tf_op jit(solution)/shard_map/ppermute | solution.py:307
  50.8 4.6 %collective-permute-start.2 = (bf16[16,32,128]{2,1,0:T(8,128)(2,1)S(1)}, bf16[16,32,128]{2,1,0:T(8,128)(2,1)S(1)}, u32[]{:S(2)}, u32[]{:S(2)}) collective-permute-start(bf16[16,32,128]{2,1,0:T(8,128)(2,1)S(1)} %fusion.1), channel_id=1, source_target_pairs={{4,0},{5,1},{6,2},{7,3},{8,4},{9,5},{10,6},{11,7},{12,8},{13,9},{1... | collective-permute-start | bytes 393224 | tf_op jit(solution)/shard_map/ppermute | solution.py:309
  59.6 27.8 %copy-start.2 = (bf16[48,192]{1,0:T(8,128)(2,1)S(1)}, bf16[48,192]{1,0:T(8,128)(2,1)}, u32[]{:S(2)}) copy-start(bf16[48,192]{1,0:T(8,128)(2,1)} %constant.50.clone.pick_ref) | copy-start | bytes 55300
  65.7 21.7 %all-to-all-start.1 = ((bf16[64,24,128]{2,1,0:T(8,128)(2,1)}), bf16[64,24,128]{2,1,0:T(8,128)(2,1)S(1)}, u32[]{:S(2)}, u32[]{:S(2)}) async-start(bf16[64,24,128]{2,1,0:T(8,128)(2,1)} %bitcast.14), calls=%async_computation.1 | async-start | bytes 786432 | tf_op jit(solution)/shard_map/all_to_all | solution.py:265

commit v5 on v4

--- a/solution.py
+++ b/solution.py
@@ -130,7 +130,7 @@
 
 def outer_kernel(
     place_ref, own_ref, low_ref, high_ref, far_ref, one_ref, two_ref, w1_ref, w2_ref, b1_ref, b2_ref, head_ref,
-    out_ref, ends, edge, h2s, planes, sums, single,
+    out_ref, ends, edge, h2s, planes, sums, single, message, sems,
 ):
     block, dx, ext, start = place_ref[0], place_ref[1], place_ref[2], place_ref[3]
     not_first = jnp.where(block > 0, 1.0, 0.0)
@@ -191,8 +191,10 @@
     lane = lax.broadcasted_iota(jnp.int32, (2 * ROWS, Z), 1)
     planes[0] = jnp.zeros((LINE, ROWS, Z), F32)
     planes[XQ + 1] = jnp.zeros((LINE, ROWS, Z), F32)
-    for x in range(1, XQ + 1, 2):
-        for l in range(0, LINE, 2):
+    moved = lax.rem(lax.broadcasted_iota(jnp.int32, (ROWS, Z), 0), 9) // 3 == dx + 1
+    leaving = []
+    for l in range(0, LINE, 2):
+        for x in range(1, XQ + 1, 2):
             columns = []
             for k in (l, l + 1):
                 y = 2 * k + 1
@@ -207,12 +209,17 @@
                 total = part[2 * ROWS : 4 * ROWS] + before + after
                 planes[x, l + k] = total[:ROWS]
                 planes[x + 1, l + k] = total[ROWS:]
-    moved = lax.rem(lax.broadcasted_iota(jnp.int32, (ROWS, Z), 0), 9) // 3 == dx + 1
-    for l in range(LINE):
-        for x in range(1, XQ + 1, 2):
-            rows = [jnp.where(moved, planes[at + dx, l], planes[at, l]) for at in (x, x + 1)]
-            at = (l * XQ + x - 1) * ROWS
-            out_ref[at : at + 2 * ROWS, :] = jnp.concatenate(rows, axis=0).astype(BF)
+        for k in (l, l + 1):
+            for x in range(1, XQ + 1, 2):
+                rows = [jnp.where(moved, planes[at + dx, k], planes[at, k]) for at in (x, x + 1)]
+                at = (k * XQ + x - 1) * ROWS
+                message[at : at + 2 * ROWS, :] = jnp.concatenate(rows, axis=0).astype(BF)
+        part = pl.ds(l * XQ * ROWS, 2 * XQ * ROWS)
+        leave = pltpu.make_async_copy(message.at[part], out_ref.at[part], sems.at[l // 2])
+        leave.start()
+        leaving.append(leave)
+    for leave in leaving:
+        leave.wait()
 
 
 def finish_kernel(back_ref, pick_ref, b_ref, out_ref):
@@ -321,7 +328,7 @@
             outer_kernel,
             out_shape=jax.ShapeDtypeStruct((S * S * ROWS, Z), BF),
             in_specs=[SMEM] + [VMEM] * 11,
-            out_specs=VMEM,
+            out_specs=pl.BlockSpec(memory_space=pltpu.HBM),
             scratch_shapes=[
                 pltpu.VMEM((6, XQ, C, Z), BF),
                 pltpu.VMEM((6, XQ * C, Z), BF),
@@ -329,6 +336,8 @@
                 pltpu.VMEM((XQ + 2, LINE, ROWS, Z), F32),
                 pltpu.VMEM((2, 27 * C, 2 * Z), F32),
                 pltpu.VMEM((30 * C, 2 * Z), F32),
+                pltpu.VMEM((S * S * ROWS, Z), BF),
+                pltpu.SemaphoreType.DMA((2,)),
             ],
             compiler_params=pltpu.CompilerParams(vmem_limit_bytes=32 << 20),
             cost_estimate=pl.CostEstimate(flops=5000000000, bytes_accessed=7000000, transcendentals=0),

time: 88.6 us -> 88.6 us (level)
  no operation moved by 1% of the time
where the time goes in v5:
time: 88.6 us; the launch traced here: 88.2 us
  waiting for transfers between devices  47.3 us (53%)
  starting transfers between devices  23.9 us (27%)
  Pallas kernels  14 us (16%)
  local copies, waits for them, and re-layouts  1.74 us (2%)
  between operations  0.97 us (1%)
    all_to_all x2, waiting for transfers between devices, swap(): lax.all_to_all(value, axes, 0, 0, tiled=True, axis_index_groups=groups)  43.1 us
    all_to_all x2, starting transfers between devices, swap(): lax.all_to_all(value, axes, 0, 0, tiled=True, axis_index_groups=groups)  18.7 us
    pallas_call x1, Pallas kernels, body(): pl.pallas_call(outer_kernel, out_shape=jax.ShapeDtypeStruct((S * S * ROWS...  5.96 us
    ppermute x1, waiting for transfers between devices, body(): lax.ppermute(own[0], 'crosslin', [(i + LINE, i) for i in range(steps - LI...  4.18 us
    pallas_call x1, Pallas kernels, body(): pl.pallas_call(inner_kernel, out_shape=[jax.ShapeDtypeStruct((6, XQ * C,...  3.94 us
    ppermute x1, starting transfers between devices, body(): lax.ppermute(own[3], 'crosslin', [(i, i + LINE) for i in range(steps - LI...  3.26 us
    pallas_call x1, Pallas kernels, body(): pl.pallas_call(split_kernel, out_shape=jax.ShapeDtypeStruct((S * S, 2 * C...  2.48 us
  transfers between devices with their start and end apart: 5, of which 3 were waited for; matrix products, arithmetic and copies ran while one was open for 1% of the time, Pallas kernels for 5%

profile of v5, /device:TPU:1, one launch (start us, length us, event | category | flops | bytes accessed | tf_op | source)
XLA Modules:
  0.0 88.2 jit_solution(4346141443999465959)
XLA Ops:
  0.0 2.5 %shard_map.82 = bf16[64,64,128]{2,1,0:T(8,128)(2,1)} custom-call(bf16[32,8,16,128]{3,2,1,0:T(8,128)(2,1)} %in_ref.1), custom_call_target="tpu_custom_call" | custom-call | tf_op jit(solution)/shard_map/pallas_call | solution.py:280
  2.5 0.0 copy-start.5
  2.5 0.0 copy-start
  2.5 0.0 copy-start.1
  2.5 0.0 copy-start.6
  2.5 0.0 copy-start.7
  2.6 13.3 %all-to-all-start = ((bf16[64,64,128]{2,1,0:T(8,128)(2,1)}), bf16[64,64,128]{2,1,0:T(8,128)(2,1)S(1)}, u32[]{:S(2)}, u32[]{:S(2)}) async-start(bf16[64,64,128]{2,1,0:T(8,128)(2,1)} %shard_map.82), calls=%async_computation | async-start | bytes 2097152 | tf_op jit(solution)/shard_map/all_to_all | solution.py:272
  15.9 0.1 select_select_fusion
  16.0 0.1 fusion.2
  16.1 0.1 mul.24
  16.2 0.1 mul.25
  16.3 0.1 mul.28
  16.4 0.1 pad_bitcast_fusion.1
  16.6 0.0 copy-done
  16.6 0.0 copy-done.1
  16.6 0.7 shard_map.83
  17.4 1.1 %copy-done.3 = bf16[960,768]{1,0:T(8,128)(2,1)} copy-done((bf16[960,768]{1,0:T(8,128)(2,1)}, bf16[960,768]{1,0:T(8,128)(2,1)S(1)}, u32[]{:S(2)}) %copy-start.3) | copy-done | bytes 1474584
  18.5 0.1 pad_add_fusion.place_ref
  18.6 27.4 %all-to-all-done = bf16[64,64,128]{2,1,0:T(8,128)(2,1)S(1)} async-done(((bf16[64,64,128]{2,1,0:T(8,128)(2,1)}), bf16[64,64,128]{2,1,0:T(8,128)(2,1)S(1)}, u32[]{:S(2)}, u32[]{:S(2)}) %all-to-all-start) | async-done | bytes 1048608 | tf_op jit(solution)/shard_map/all_to_all | solution.py:272
  46.0 0.1 broadcast_in_dim.71.b1_ref
  46.1 0.1 broadcast_in_dim.72.b2_ref
  46.2 3.3 %collective-permute-start = (bf16[16,2,32,128]{3,2,1,0:T(8,128)(2,1)S(1)}, bf16[16,2,32,128]{3,2,1,0:T(8,128)(2,1)S(1)}, u32[]{:S(2)}, u32[]{:S(2)}) collective-permute-start(bf16[16,2,32,128]{3,2,1,0:T(8,128)(2,1)S(1)} %bitcast.37), channel_id=1, source_target_pairs={{0,4},{1,5},{2,6},{3,7},{4,8},{5,9},{6,10},{7,11},{8,12},{9,13},{1... | collective-permute-start | bytes 786440 | tf_op jit(solution)/shard_map/ppermute | solution.py:315
  49.5 1.3 %collective-permute-start.1 = (bf16[16,2,32,128]{3,2,1,0:T(8,128)(2,1)S(1)}, bf16[16,2,32,128]{3,2,1,0:T(8,128)(2,1)S(1)}, u32[]{:S(2)}, u32[]{:S(2)}) collective-permute-start(bf16[16,2,32,128]{3,2,1,0:T(8,128)(2,1)S(1)} %bitcast.36), channel_id=1, source_target_pairs={{4,0},{5,1},{6,2},{7,3},{8,4},{9,5},{10,6},{11,7},{12,8},{13,9},{1... | collective-permute-start | bytes 786440 | tf_op jit(solution)/shard_map/ppermute | solution.py:314
  50.8 0.7 collective-permute-start.2
  51.5 3.9 %shard_map.84 = (bf16[6,512,128]{2,1,0:T(8,128)(2,1)S(1)}, bf16[16,4,32,128]{3,2,1,0:T(8,128)(2,1)S(1)}) custom-call(bf16[4,16,2,32,128]{4,3,2,1,0:T(8,128)(2,1)S(1)} %bitcast.30, bf16[960,768]{1,0:T(8,128)(2,1)S(1)} %get-tuple-element.20.w1_ref, bf16[960,768]{1,0:T(8,128)(2,1)S(1)} %copy-done.4, f32[32,128]{1,0:T(8,128)S(1)} %broadcast_in_dim.71.b1_ref, ...), custom_call_target="tpu_custom_call" | custom-call | flops 4000000000 | bytes 6000000 | tf_op jit(solution)/shard_map/pallas_call | solution.py:318
  55.4 0.0 collective-permute-done.2.far_ref
  55.4 0.0 collective-permute-done.low_ref
  55.4 4.2 %collective-permute-done.1.high_ref = bf16[16,2,32,128]{3,2,1,0:T(8,128)(2,1)S(1)} collective-permute-done((bf16[16,2,32,128]{3,2,1,0:T(8,128)(2,1)S(1)}, bf16[16,2,32,128]{3,2,1,0:T(8,128)(2,1)S(1)}, u32[]{:S(2)}, u32[]{:S(2)}) %collective-permute-start.1) | collective-permute-done | bytes 262176 | tf_op jit(solution)/shard_map/ppermute | solution.py:314
  59.6 6.0 %shard_map.85 = bf16[1536,128]{1,0:T(8,128)(2,1)} custom-call(s32[4]{0:T(128)S(1)} %pad_add_fusion.place_ref, bf16[4,16,2,32,128]{4,3,2,1,0:T(8,128)(2,1)S(1)} %bitcast.31, bf16[16,2,32,128]{3,2,1,0:T(8,128)(2,1)S(1)} %collective-permute-done.low_ref, bf16[16,2,32,128]{3,2,1,0:T(8,128)(2,1)S(1)} %collective-permute-done.1.high_ref, ...), custom_call_target="tpu_custom_call" | custom-call | flops 5000000000 | bytes 7000000 | tf_op jit(solution)/shard_map/pallas_call | solution.py:327
  65.6 5.4 %all-to-all-start.1 = ((bf16[64,24,128]{2,1,0:T(8,128)(2,1)}), bf16[64,24,128]{2,1,0:T(8,128)(2,1)S(1)}, u32[]{:S(2)}, u32[]{:S(2)}) async-start(bf16[64,24,128]{2,1,0:T(8,128)(2,1)} %bitcast.14), calls=%async_computation.1 | async-start | bytes 786432 | tf_op jit(solution)/shard_map/all_to_all | solution.py:272
  71.6 15.7 %all-to-all-done.1 = bf16[64,24,128]{2,1,0:T(8,128)(2,1)S(1)} async-done(((bf16[64,24,128]{2,1,0:T(8,128)(2,1)}), bf16[64,24,128]{2,1,0:T(8,128)(2,1)S(1)}, u32[]{:S(2)}, u32[]{:S(2)}) %all-to-all-start.1) | async-done | bytes 393248 | tf_op jit(solution)/shard_map/all_to_all | solution.py:272
  87.3 0.9 %shard_map.86 = f32[8,16,128]{2,1,0:T(8,128)} custom-call(bf16[1536,128]{1,0:T(8,128)(2,1)S(1)} %bitcast.32, bf16[48,192]{1,0:T(8,128)(2,1)S(1)} %copy-done.2, f32[1]{0:T(128)S(6)} %copy.19.b_ref), custom_call_target="tpu_custom_call" | custom-call | tf_op jit(solution)/shard_map/pallas_call | solution.py:347
  (18 shorter events, 0.1 us)
Async XLA Ops:
  2.5 13.8 %copy-start.5 = (bf16[3,3,3,32]{3,2,1,0:T(4,128)(2,1)S(1)}, bf16[3,3,3,32]{3,2,1,0:T(4,128)(2,1)}, u32[]{:S(2)}) copy-start(bf16[3,3,3,32]{3,2,1,0:T(4,128)(2,1)} %param.13) | copy-start | bytes 5188
  2.5 14.1 %copy-start = (bf16[3,3,3,32,32]{4,3,2,1,0:T(8,128)(2,1)S(1)}, bf16[3,3,3,32,32]{4,3,2,1,0:T(8,128)(2,1)}, u32[]{:S(2)}) copy-start(bf16[3,3,3,32,32]{4,3,2,1,0:T(8,128)(2,1)} %param.9) | copy-start | bytes 165892
  2.5 14.1 %copy-start.1 = (bf16[3,3,3,32,32]{4,3,2,1,0:T(8,128)(2,1)S(1)}, bf16[3,3,3,32,32]{4,3,2,1,0:T(8,128)(2,1)}, u32[]{:S(2)}) copy-start(bf16[3,3,3,32,32]{4,3,2,1,0:T(8,128)(2,1)} %param.11) | copy-start | bytes 165892
  2.5 43.5 %copy-start.6 = (f32[32]{0:T(128)S(1)}, f32[32]{0:T(128)}, u32[]{:S(2)}) copy-start(f32[32]{0:T(128)} %param.10) | copy-start | bytes 388
  2.5 43.5 %copy-start.7 = (f32[32]{0:T(128)S(1)}, f32[32]{0:T(128)}, u32[]{:S(2)}) copy-start(f32[32]{0:T(128)} %param.12) | copy-start | bytes 388
  2.6 43.4 %all-to-all-start = ((bf16[64,64,128]{2,1,0:T(8,128)(2,1)}), bf16[64,64,128]{2,1,0:T(8,128)(2,1)S(1)}, u32[]{:S(2)}, u32[]{:S(2)}) async-start(bf16[64,64,128]{2,1,0:T(8,128)(2,1)} %shard_map.82), calls=%async_computation | async-start | bytes 2097152 | tf_op jit(solution)/shard_map/all_to_all | solution.py:272
  17.3 1.1 %copy-start.3 = (bf16[960,768]{1,0:T(8,128)(2,1)}, bf16[960,768]{1,0:T(8,128)(2,1)S(1)}, u32[]{:S(2)}) copy-start(bf16[960,768]{1,0:T(8,128)(2,1)S(1)} %get-tuple-element.21.w2_ref) | copy-start | bytes 4423684
  46.0 5.5 %copy-start.4 = (bf16[960,768]{1,0:T(8,128)(2,1)S(1)}, bf16[960,768]{1,0:T(8,128)(2,1)}, u32[]{:S(2)}) copy-start(bf16[960,768]{1,0:T(8,128)(2,1)} %copy-done.3) | copy-start | bytes 4423684
  46.2 9.2 %collective-permute-start = (bf16[16,2,32,128]{3,2,1,0:T(8,128)(2,1)S(1)}, bf16[16,2,32,128]{3,2,1,0:T(8,128)(2,1)S(1)}, u32[]{:S(2)}, u32[]{:S(2)}) collective-permute-start(bf16[16,2,32,128]{3,2,1,0:T(8,128)(2,1)S(1)} %bitcast.37), channel_id=1, source_target_pairs={{0,4},{1,5},{2,6},{3,7},{4,8},{5,9},{6,10},{7,11},{8,12},{9,13},{1... | collective-permute-start | bytes 786440 | tf_op jit(solution)/shard_map/ppermute | solution.py:315
  49.5 10.2 %collective-permute-start.1 = (bf16[16,2,32,128]{3,2,1,0:T(8,128)(2,1)S(1)}, bf16[16,2,32,128]{3,2,1,0:T(8,128)(2,1)S(1)}, u32[]{:S(2)}, u32[]{:S(2)}) collective-permute-start(bf16[16,2,32,128]{3,2,1,0:T(8,128)(2,1)S(1)} %bitcast.36), channel_id=1, source_target_pairs={{4,0},{5,1},{6,2},{7,3},{8,4},{9,5},{10,6},{11,7},{12,8},{13,9},{1... | collective-permute-start | bytes 786440 | tf_op jit(solution)/shard_map/ppermute | solution.py:314
  50.8 4.6 %collective-permute-start.2 = (bf16[16,32,128]{2,1,0:T(8,128)(2,1)S(1)}, bf16[16,32,128]{2,1,0:T(8,128)(2,1)S(1)}, u32[]{:S(2)}, u32[]{:S(2)}) collective-permute-start(bf16[16,32,128]{2,1,0:T(8,128)(2,1)S(1)} %fusion.1), channel_id=1, source_target_pairs={{4,0},{5,1},{6,2},{7,3},{8,4},{9,5},{10,6},{11,7},{12,8},{13,9},{1... | collective-permute-start | bytes 393224 | tf_op jit(solution)/shard_map/ppermute | solution.py:316
  59.6 27.7 %copy-start.2 = (bf16[48,192]{1,0:T(8,128)(2,1)S(1)}, bf16[48,192]{1,0:T(8,128)(2,1)}, u32[]{:S(2)}) copy-start(bf16[48,192]{1,0:T(8,128)(2,1)} %constant.50.clone.pick_ref) | copy-start | bytes 55300
  65.6 21.7 %all-to-all-start.1 = ((bf16[64,24,128]{2,1,0:T(8,128)(2,1)}), bf16[64,24,128]{2,1,0:T(8,128)(2,1)S(1)}, u32[]{:S(2)}, u32[]{:S(2)}) async-start(bf16[64,24,128]{2,1,0:T(8,128)(2,1)} %bitcast.14), calls=%async_computation.1 | async-start | bytes 786432 | tf_op jit(solution)/shard_map/all_to_all | solution.py:272
